TPU v7x, 32 devices: a whole 2x2x4 slice. The times are simulated.
32 devices in a mesh: mode: 8 (over z, y), gz: 4 (over x, core).
Axes of the slice: x: 2, y: 2, z: 4, core: 2. Of those that a mesh axis runs over, the one named last changes fastest.
Arguments:
- efield: float32 [3, 256, 64, 256], P(None, 'mode', 'gz'), may hold values from -0.6 to 0.6
- hfield: float32 [3, 256, 64, 256], P(None, 'mode', 'gz'), may hold values from -0.6 to 0.6
- polar: float32 [3, 4, 16, 256, 512], P(None, 'gz', 'mode'), may hold values from -1.2 to 1.2
- velocity: float32 [3, 4, 16, 256, 512], P(None, 'gz', 'mode'), may hold values from -0.5 to 0.5
- material: float32 [4, 4, 16, 256], P(None, 'gz', 'mode'), may hold values from 0.05 to 0.5
Outputs:
- new_efield: float32 [3, 256, 64, 256], P(None, 'mode', 'gz')
- new_hfield: float32 [3, 256, 64, 256], P(None, 'mode', 'gz')
- new_polar: float32 [3, 4, 16, 256, 512], P(None, 'gz', 'mode')
- new_velocity: float32 [3, 4, 16, 256, 512], P(None, 'gz', 'mode')
All inputs are finite; a program needn't handle non-finite values.
Results may differ from a plain program's by a relative error of at most 0.0001.
Values sent between devices are 32-bit elements; how exact they have to be, the bound alone decides.
No kernel may reach another device: no remote copies, remote signals or barrier semaphores. Data moves between devices by JAX's collectives and lax.ppermute only.
A program may use at most 64 MiB of HBM per device.

v0:
```python
import functools
import math

import jax
import jax.numpy as jnp
from jax import lax
from jax.experimental import pallas as pl
from jax.experimental.pallas import tpu as pltpu
from jax.sharding import PartitionSpec as P


SUBSTEPS = 4
LANES = 128
RATIO = 0.5


def distances(peers):
    quarter = peers // 4
    far, near = list(range(3 * quarter, peers)), list(range(1, quarter))
    middle = list(range(3 * quarter - 1, quarter - 1, -1))
    far.reverse()
    inner, outer = far[:1] + far[1:] + near, near[:1] + far[1:] + far[:1] + near[1:]
    return inner + middle + [0], outer + middle + [0]


def peer(me, s, peers):
    inner, outer = (by_class[s] for by_class in distances(peers))
    if inner == outer:
        return me ^ inner
    return me ^ jnp.where(is_inner(me, peers), inner, outer)


def is_inner(me, peers):
    quarter = peers // 4
    return (me >= quarter) & (me < 3 * quarter)


def tables(modes, angles):
    order = jnp.arange(modes, dtype=jnp.int32) // 2
    parity = jnp.arange(modes, dtype=jnp.int32) % 2
    steps = jnp.arange(angles, dtype=jnp.int32)
    phase = order[:, None] * steps[None, :] % angles
    theta = phase.astype(jnp.float32) * (2.0 * math.pi / angles)
    return jnp.where(parity[:, None] == 0, jnp.cos(theta), jnp.sin(theta))


def split(value):
    high = value.astype(jnp.bfloat16)
    return high, (value - high.astype(jnp.float32)).astype(jnp.bfloat16)


class Plane:
    def __init__(self, first, modes, radii, total):
        row = lax.broadcasted_iota(jnp.int32, (modes, radii), 0)
        self.lane = lax.broadcasted_iota(jnp.int32, (modes, radii), 1)
        self.even = row % 2 == 0
        order = ((first + row) // 2).astype(jnp.float32)
        self.signed = jnp.where(self.even, order, -order)
        self.modes, self.radii = modes, radii
        self.time_step = 0.7 / total
        place = self.lane.astype(jnp.float32)
        self.outer = place + 1.0
        self.inner = place + 0.5
        self.per_outer = 1.0 / self.outer
        self.per_inner = 1.0 / self.inner

    def rotate(self, x):
        swapped = jnp.where(
            self.even, pltpu.roll(x, self.modes - 1, 0), pltpu.roll(x, 1, 0)
        )
        return self.signed * swapped

    def down(self, x):
        return x - jnp.where(self.lane == 0, 0.0, pltpu.roll(x, 1, 1))

    def up(self, x):
        return jnp.where(self.lane == self.radii - 1, 0.0, pltpu.roll(x, self.radii - 1, 1)) - x

    def magnetic(self, e, e_above, h):
        ts = self.time_step
        return (
            h[0] - (ts * self.per_outer) * self.rotate(e[2]) + RATIO * (e_above[1] - e[1]),
            h[1] - RATIO * (e_above[0] - e[0]) + ts * self.down(e[2]),
            h[2] - (ts * self.per_inner) * (self.down(self.outer * e[1]) - self.rotate(e[0])),
        )

    def curl(self, h, h_below):
        ts = self.time_step
        return (
            (ts * self.per_inner) * self.rotate(h[2]) - RATIO * (h[1] - h_below[1]),
            RATIO * (h[0] - h_below[0]) - ts * self.up(h[2]),
            (ts * self.per_outer) * (self.up(self.inner * h[1]) - self.rotate(h[0])),
        )


def to_zk(source, target):
    count, modes, planes, _ = source.shape
    for c in range(count):
        for k in range(0, modes, 8):
            for z in range(0, planes, 8):
                target[c, z : z + 8, k : k + 8, :] = jnp.swapaxes(
                    source[c, k : k + 8, z : z + 8, :], 0, 1
                )


def to_kz(source, target):
    count, planes, modes, _ = source.shape
    for c in range(count):
        for k in range(0, modes, 8):
            for z in range(0, planes, 8):
                target[c, k : k + 8, z : z + 8, :] = jnp.swapaxes(
                    source[c, z : z + 8, k : k + 8, :], 0, 1
                )


def pack_kernel(e_kz, h_kz, *refs):
    outs, (held, e_zk, tail, h_last, in_sem, out_sem, edge_sem) = refs[:-7], refs[-7:]
    blocks, (to_lower, to_upper) = outs[:-2], outs[-2:]
    peers = len(blocks)
    depth = e_zk.shape[1]
    planes = depth // peers
    me = lax.axis_index("mode")
    loads = [pltpu.make_async_copy(e_kz.at[c], held.at[c], in_sem.at[c]) for c in range(3)]
    loads.append(pltpu.make_async_copy(h_kz.at[:, :, pl.ds(depth - 8, 8)], tail, in_sem.at[3]))
    for load in loads:
        load.start()
    stores = []

    def store(source, target, semaphore):
        stores.append(pltpu.make_async_copy(source, target, semaphore))
        stores[-1].start()

    for c in range(3):
        loads[c].wait()
        to_zk(held.at[pl.ds(c, 1)], e_zk.at[pl.ds(c, 1)])
        for s in range(peers):
            first = peer(me, s, peers) * planes
            store(
                e_zk.at[c, pl.ds(first, planes)], blocks[s].at[pl.ds(c * planes, planes)], out_sem.at[c, s]
            )
    store(e_zk.at[:, 0], to_lower, edge_sem.at[0])
    store(e_zk.at[:, depth - 1], to_upper.at[0], edge_sem.at[1])
    loads[3].wait()
    for c in range(3):
        h_last[c] = tail[c, :, 7, :]
    store(h_last, to_upper.at[1], edge_sem.at[2])
    for copy in stores:
        copy.wait()


def unpack_kernel(ahead, h_zk, *refs):
    blocks, (e_zk, to_lower, to_upper) = refs[:-3], refs[-3:]
    peers = len(blocks)
    me = lax.axis_index("mode")
    planes = e_zk.shape[1] // peers
    last = e_zk.shape[1] - 1
    for s in range(peers):
        first = peer(me, s, peers) * planes
        for c in range(2):
            for q in range(planes):
                e_zk[c, first + q] = ahead[c, first + q] - blocks[s][c * planes + q]
        for q in range(planes - 1):
            e_zk[2, first + q] = ahead[2, first + q]
        e_zk[2, first + planes - 1] = ahead[2, first + planes - 1] - blocks[s][2 * planes]
    for c in range(3):
        to_lower[c] = e_zk[c, 0]
        to_upper[0, c] = e_zk[c, last]
        to_upper[1, c] = h_zk[c, last]


def advance(peers, e, base, h, above, below, h_new, store):
    planes, modes, radii = e.shape[1:]
    op = Plane(lax.axis_index("mode") * modes, modes, radii, modes * peers)

    def magnetic(z, e_above):
        new = op.magnetic([e[c, z] for c in range(3)], e_above, [h[c, z] for c in range(3)])
        for c in range(3):
            h_new[c, z] = new[c]

    def loop_h(z, carry):
        magnetic(z, [e[c, z + 1] for c in range(2)])
        return carry

    lax.fori_loop(0, planes - 1, loop_h, 0)
    magnetic(planes - 1, [above[c] for c in range(2)])
    edge = op.magnetic(
        [below[0, c] for c in range(3)], [e[c, 0] for c in range(2)], [below[1, c] for c in range(3)]
    )
    inside = lax.axis_index("gz") > 0
    edge = [jnp.where(inside, edge[c], 0.0) for c in range(2)]

    def electric(z, h_below):
        curl = op.curl([h_new[c, z] for c in range(3)], h_below)
        store(z, curl, [base[c, z] for c in range(3)])

    electric(0, edge)

    def loop_e(z, carry):
        electric(z, [h_new[c, z - 1] for c in range(2)])
        return carry

    lax.fori_loop(1, planes, loop_e, 0)


def first_kernel(e_kz, h_kz, above, below, *refs):
    e_zk, h_zk, curl = refs[-3:]
    blocks, (ahead, h_new) = refs[:-5], refs[-5:-3]
    peers = len(blocks)
    me = lax.axis_index("mode")
    to_zk(e_kz, e_zk)
    to_zk(h_kz, h_zk)

    def store(z, found, base):
        for c in range(3):
            curl[c, z] = found[c]
            ahead[c, z] = base[c] + found[c]

    advance(peers, e_zk, e_zk, h_zk, above, below, h_new, store)
    planes = e_zk.shape[1] // peers
    for s in range(peers):
        first = peer(me, s, peers) * planes
        for c in range(2):
            for q in range(planes):
                blocks[s][c * planes + q] = curl[c, first + q]
        blocks[s][2 * planes] = curl[2, first]


def last_kernel(peers, e_zk, ahead, h_zk, above, below, ahead_new, h_kz, h_new):
    def store(z, found, base):
        for c in range(3):
            ahead_new[c, z] = base[c] + found[c]

    advance(peers, e_zk, ahead, h_zk, above, below, h_new, store)
    to_kz(h_new, h_kz)


def finish_kernel(ahead, *refs):
    blocks, (e_kz, e_zk, done, out_sem) = refs[:-4], refs[-4:]
    peers = len(blocks)
    planes = e_zk.shape[1] // peers
    stores = []
    for c in range(3):
        for s in range(peers):
            first = peer(lax.axis_index("mode"), s, peers) * planes
            for q in range(planes):
                e_zk[c, first + q] = ahead[c, first + q] - blocks[s][c * planes + q]
        to_kz(e_zk.at[pl.ds(c, 1)], done.at[pl.ds(c, 1)])
        stores.append(pltpu.make_async_copy(done.at[c], e_kz.at[c], out_sem.at[c]))
        stores[-1].start()
    for copy in stores:
        copy.wait()


def respond(table, fields, points, polar, velocity, coefficient, new_polar, new_velocity, store, q, base):
    high, low = table
    rows, angles = points.shape[1:]
    for c in range(3):
        f_high, f_low = split(fields(c).T)
        points[c] = (
            jnp.dot(f_high, high[...], preferred_element_type=jnp.float32)
            + jnp.dot(f_high, low[...], preferred_element_type=jnp.float32)
            + jnp.dot(f_low, high[...], preferred_element_type=jnp.float32)
        )
    width = min(angles, 256)

    def loop(g, carry):
        at = pl.ds(pl.multiple_of(g * 8, 8), 8)
        there = pl.ds(pl.multiple_of(base + g * 8, 8), 8)
        keep, push, spring, hard = [
            jnp.broadcast_to(coefficient[q, there, n : n + 1], (8, width)) for n in range(4)
        ]
        for start in range(0, angles, width):
            part = slice(start, start + width)
            before = [polar[c, 0, q, there, part] for c in range(3)]
            v = [velocity[c, 0, q, there, part] for c in range(3)]
            drive = [push * points[c, at, part] for c in range(3)]
            p = before
            for _ in range(SUBSTEPS):
                energy = p[0] * p[0] + p[1] * p[1] + p[2] * p[2]
                pull = spring + hard * energy
                v = [keep * v[c] + (drive[c] - pull * p[c]) for c in range(3)]
                p = [p[c] + v[c] for c in range(3)]
            for c in range(3):
                new_polar[c, 0, q, there, part] = p[c]
                new_velocity[c, 0, q, there, part] = v[c]
                points[c, at, part] = p[c] - before[c]
        return carry

    lax.fori_loop(0, rows // 8, loop, 0, unroll=2)
    modes = high.shape[0]
    weight = jnp.where(
        lax.broadcasted_iota(jnp.int32, (modes, rows), 0) == 0, 1.0 / angles, 2.0 / angles
    )
    contract = (((1,), (1,)), ((), ()))
    for c in range(3):
        c_high, c_low = split(points[c])
        modal = (
            lax.dot_general(high[...], c_high, contract, preferred_element_type=jnp.float32)
            + lax.dot_general(low[...], c_high, contract, preferred_element_type=jnp.float32)
            + lax.dot_general(high[...], c_low, contract, preferred_element_type=jnp.float32)
        )
        store(c, weight * modal)


def gas_step(fields, points, high, low, polar, velocity, coefficient, new_polar, new_velocity, change):
    planes = coefficient.shape[0]
    rows = points.shape[1]
    parts = coefficient.shape[1] // rows

    def chunk(n, carry):
        q, base = n // parts, pl.multiple_of(n % parts * rows, rows)
        at = pl.ds(base, rows)

        def store(c, modal):
            change[c * planes + q, :, at] = modal

        respond(
            (high, low), lambda c: fields[c * planes + q, :, at], points,
            polar, velocity, coefficient, new_polar, new_velocity, store, q, base,
        )
        return carry

    lax.fori_loop(0, planes * parts, chunk, 0)


def gas_first_kernel(peers, planes, basis, coefficient, polar, velocity, *refs):
    arrived, refs = refs[:peers], refs[peers:]
    blocks, refs = refs[:peers], refs[peers:]
    new_polar, new_velocity, change, rest, fields, points, high, low = refs
    me = lax.axis_index("mode")
    modes, radii = arrived[0].shape[1:]

    high[...], low[...] = split(basis[...])
    for s in range(peers):
        at = pl.ds(pl.multiple_of(peer(me, s, peers) * modes, modes), modes)
        for n in range(3 * planes):
            fields[n, at, :] = arrived[s][n]

    gas_step(fields, points, high, low, polar, velocity, coefficient, new_polar, new_velocity, change)

    for s in range(peers):
        first = peer(me, s, peers) * modes
        at = pl.ds(pl.multiple_of(first, modes), modes)
        op = Plane(first, modes, radii, modes * peers)
        for n in range(3 * planes):
            rest[n, at, :] = fields[n, at, :] - change[n, at, :]
        phi, axial = None, change[2 * planes, at, :]
        for q in range(planes):
            for c in range(2):
                sent = change[c * planes + q, at, :]
                if phi is not None:
                    sent = sent + (op.down(phi) if c == 0 else op.per_outer * op.rotate(phi))
                blocks[s][c * planes + q] = sent
            if q < planes - 1:
                phi = (-op.time_step / RATIO) * axial
                axial = axial + change[2 * planes + q + 1, at, :]
        blocks[s][2 * planes] = axial


def gas_last_kernel(peers, planes, basis, coefficient, polar, velocity, rest, earlier, *refs):
    arrived, refs = refs[:peers], refs[peers:]
    blocks, refs = refs[:peers], refs[peers:]
    new_polar, new_velocity, fields, points, change, high, low = refs
    me = lax.axis_index("mode")
    modes, radii = arrived[0].shape[1:]

    high[...], low[...] = split(basis[...])
    for s in range(peers):
        first = peer(me, s, peers) * modes
        at = pl.ds(pl.multiple_of(first, modes), modes)
        op = Plane(first, modes, radii, modes * peers)
        axial = arrived[s][2 * planes]
        for q in range(planes):
            radial, azimuth = arrived[s][q], arrived[s][planes + q]
            if q > 0:
                flux = op.up(op.inner * radial) + op.rotate(azimuth)
                axial = axial - (op.time_step / RATIO) * op.per_outer * flux
            for c, found in enumerate((radial, azimuth, axial)):
                n = c * planes + q
                fields[n, at, :] = rest[n, at, :] + found

    gas_step(fields, points, high, low, polar, velocity, coefficient, new_polar, new_velocity, change)

    for s in range(peers):
        at = pl.ds(pl.multiple_of(peer(me, s, peers) * modes, modes), modes)
        for n in range(3 * planes):
            blocks[s][n] = earlier[n, at, :] + change[n, at, :]


def f32(*shape):
    return jax.ShapeDtypeStruct(shape, jnp.float32)


def grant(*sizes):
    return pltpu.CompilerParams(vmem_limit_bytes=sum(sizes) * 5 // 4 + (1 << 20))


def nbytes(x):
    return 4 * math.prod(x if isinstance(x, tuple) else x.shape)


def call(kernel, out, *operands, scratch=(), tables=(), semaphores=(), flops=0, reads=pltpu.VMEM, writes=pltpu.VMEM, room=True):
    moved = sum(4 * math.prod(x.shape) for x in (*operands, *out))
    return pl.pallas_call(
        kernel,
        out_shape=out,
        in_specs=[pl.BlockSpec(memory_space=reads)] * len(operands),
        out_specs=[pl.BlockSpec(memory_space=writes)] * len(out),
        scratch_shapes=[pltpu.VMEM(shape, jnp.float32) for shape in scratch]
        + [pltpu.VMEM(shape, jnp.bfloat16) for shape in tables]
        + [pltpu.SemaphoreType.DMA(shape) for shape in semaphores],
        cost_estimate=pl.CostEstimate(flops=flops, bytes_accessed=moved, transcendentals=0),
        compiler_params=grant(*map(nbytes, (*operands, *out, *scratch, *tables))) if room else None,
    )(*operands)


def gas_call(kernel, basis, coefficient, polar, velocity, extra, arrived, blocks, kept, planes):
    modes, angles = basis.shape
    radii = polar.shape[3]
    rows = min(radii, LANES)
    held = (3 * planes, modes, radii)
    return call(
        functools.partial(kernel, len(arrived), planes),
        [*blocks, f32(*polar.shape), f32(*velocity.shape), *kept],
        basis, coefficient, polar, velocity, *extra, *arrived,
        scratch=[held, (3, rows, angles)] + ([] if kept else [held]), tables=[(modes, angles)] * 2,
        flops=12 * 3 * planes * radii * modes * angles,
    )


def exchange(blocks):
    peers = len(blocks)
    moved = []
    for s in range(peers - 1):
        inner, outer = (by_class[s] for by_class in distances(peers))
        pairs = [(i, i ^ (inner if is_inner(i, peers) else outer)) for i in range(peers)]
        moved.append(lax.ppermute(blocks[s], "mode", pairs))
    return moved + blocks[-1:]


def along(value, steps):
    count = lax.axis_size("gz")
    first, last = max(0, -steps), min(count, count - steps)
    return lax.ppermute(value, "gz", [(i, i + steps) for i in range(first, last)])


def run(efield, hfield, polar, velocity, material):
    peers = lax.axis_size("mode")
    _, modes, depth, radii = efield.shape
    planes = depth // peers
    angles = polar.shape[4]
    electric = [f32(3 * planes, modes, radii)] * peers
    curled = [f32(2 * planes + 1, modes, radii)] * peers
    zk = f32(3, depth, modes, radii)
    kz = f32(3, modes, depth, radii)
    lower, upper = f32(3, modes, radii), f32(2, 3, modes, radii)

    *blocks, to_lower, to_upper = call(
        pack_kernel, [*electric, lower, upper], efield, hfield,
        scratch=[kz.shape, zk.shape, (3, modes, 8, radii), lower.shape],
        semaphores=[(4,), (3, peers), (3,)], reads=pl.ANY, writes=pl.ANY, room=False,
    )
    arrived = exchange(blocks)
    above, below = along(to_lower, -1), along(to_upper, 1)

    stiff, damp, couple, harden = [material[n, 0] for n in range(4)]
    scale = 1.0 / (1.0 + 0.5 * damp)
    coefficient = jnp.stack(
        [(1.0 - 0.5 * damp) * scale, stiff * couple * scale, stiff * scale, 0.1 * harden * scale], axis=-1
    )
    basis = tables(modes * peers, angles)

    *curl_blocks, ahead, h_zk = call(
        first_kernel, [*curled, zk, zk], efield, hfield, above, below,
        scratch=[zk.shape, zk.shape, zk.shape],
    )
    curl_arrived = exchange(curl_blocks)

    held = f32(3 * planes, modes * peers, radii)
    *back, polar, velocity, change, rest = gas_call(
        gas_first_kernel, basis, coefficient, polar, velocity,
        [], arrived, curled, [held, held], planes,
    )
    returned = exchange(back)
    *back, polar, velocity = gas_call(
        gas_last_kernel, basis, coefficient, polar, velocity,
        [rest, change], curl_arrived, electric, [], planes,
    )
    total = exchange(back)

    e_zk, to_lower, to_upper = call(unpack_kernel, [zk, lower, upper], ahead, h_zk, *returned)
    above, below = along(to_lower, -1), along(to_upper, 1)
    ahead, new_hfield = call(
        functools.partial(last_kernel, peers), [zk, kz], e_zk, ahead, h_zk, above, below, scratch=[zk.shape]
    )
    (new_efield,) = call(
        finish_kernel, [kz], ahead, *total,
        scratch=[zk.shape, kz.shape], semaphores=[(3,)], writes=pltpu.HBM,
    )
    return new_efield, new_hfield, polar, velocity


def solution(mesh):
    field = P(None, "mode", "gz", None)
    state = P(None, "gz", "mode", None, None)
    return jax.shard_map(
        run,
        mesh=mesh,
        in_specs=(field, field, state, state, P(None, "gz", "mode", None)),
        out_specs=(field, field, state, state),
        check_vma=False,
    )
```

profile of v0, /device:TPU:0, one launch (start us, length us, event | category | flops | bytes accessed | tf_op | source)
XLA Modules:
  0.0 178.7 jit_solution(3963377508158922088)
XLA Ops:
  0.6 2.7 %shard_map.84 = (f32[6,32,256]{2,1,0:T(8,128)}, f32[6,32,256]{2,1,0:T(8,128)}, f32[6,32,256]{2,1,0:T(8,128)}, f32[6,32,256]{2,1,0:T(8,128)}, f32[6,32,256]{2,1,0...) custom-call(f32[3,32,16,256]{3,2,1,0:T(8,128)} %e_kz.3, ...), custom_call_target="tpu_custom_call" | custom-call | bytes 5013504 | tf_op jit(solution)/shard_map/pallas_call | solution.py:404
  4.7 3.0 %collective-permute-start.1 = (f32[2,3,32,256]{3,2,1,0:T(8,128)}, f32[2,3,32,256]{3,2,1,0:T(8,128)S(1)}, u32[]{:S(2)}, u32[]{:S(2)}) collective-permute-start(f32[2,3,32,256]{3,2,1,0:T(8,128)} %get-tuple-element.52), channel_id=1, source_target_pairs={{0,1},{1,2},{2,3},{4,5},{5,6},{6,7},{8,9},{9,10},{10,11},{12,13},{... | collective-permute-start | bytes 589832 | tf_op jit(solution)/shard_map/ppermute | solution.py:444
  7.7 3.1 %collective-permute-start.2 = (f32[6,32,256]{2,1,0:T(8,128)}, f32[6,32,256]{2,1,0:T(8,128)}, u32[]{:S(2)}, u32[]{:S(2)}) collective-permute-start(f32[6,32,256]{2,1,0:T(8,128)} %get-tuple-element.55), channel_id=1, source_target_pairs={{0,4},{4,0},{8,20},{12,16},{16,12},{20,8},{24,28},{28,24},{1,5},{5... | collective-permute-start | bytes 589832 | tf_op jit(solution)/shard_map/ppermute | solution.py:437
  10.8 3.6 %collective-permute-start.3 = (f32[6,32,256]{2,1,0:T(8,128)}, f32[6,32,256]{2,1,0:T(8,128)}, u32[]{:S(2)}, u32[]{:S(2)}) collective-permute-start(f32[6,32,256]{2,1,0:T(8,128)} %get-tuple-element.56), channel_id=1, source_target_pairs={{0,24},{4,28},{8,16},{12,20},{16,8},{20,12},{24,0},{28,4},{1,25},{... | collective-permute-start | bytes 589832 | tf_op jit(solution)/shard_map/ppermute | solution.py:437
  21.2 2.0 %collective-permute-start.5 = (f32[6,32,256]{2,1,0:T(8,128)}, f32[6,32,256]{2,1,0:T(8,128)S(1)}, u32[]{:S(2)}, u32[]{:S(2)}) collective-permute-start(f32[6,32,256]{2,1,0:T(8,128)} %get-tuple-element.58), channel_id=1, source_target_pairs={{0,20},{4,16},{8,28},{12,24},{16,4},{20,0},{24,12},{28,8},{1,21},{... | collective-permute-start | bytes 589832 | tf_op jit(solution)/shard_map/ppermute | solution.py:437
  23.2 2.1 %collective-permute-start.6 = (f32[6,32,256]{2,1,0:T(8,128)}, f32[6,32,256]{2,1,0:T(8,128)S(1)}, u32[]{:S(2)}, u32[]{:S(2)}) collective-permute-start(f32[6,32,256]{2,1,0:T(8,128)} %get-tuple-element.59), channel_id=1, source_target_pairs={{0,16},{4,20},{8,24},{12,28},{16,0},{20,4},{24,8},{28,12},{1,17},{... | collective-permute-start | bytes 589832 | tf_op jit(solution)/shard_map/ppermute | solution.py:437
  25.3 12.2 %collective-permute-start.7 = (f32[6,32,256]{2,1,0:T(8,128)}, f32[6,32,256]{2,1,0:T(8,128)S(1)}, u32[]{:S(2)}, u32[]{:S(2)}) collective-permute-start(f32[6,32,256]{2,1,0:T(8,128)} %get-tuple-element.60), channel_id=1, source_target_pairs={{0,12},{4,8},{8,4},{12,0},{16,28},{20,24},{24,20},{28,16},{1,13},{... | collective-permute-start | bytes 589832 | tf_op jit(solution)/shard_map/ppermute | solution.py:437
  37.5 3.3 %collective-permute-start.8 = (f32[6,32,256]{2,1,0:T(8,128)}, f32[6,32,256]{2,1,0:T(8,128)S(1)}, u32[]{:S(2)}, u32[]{:S(2)}) collective-permute-start(f32[6,32,256]{2,1,0:T(8,128)} %get-tuple-element.61), channel_id=1, source_target_pairs={{0,8},{4,12},{8,0},{12,4},{16,24},{20,28},{24,16},{28,20},{1,9},{5... | collective-permute-start | bytes 589832 | tf_op jit(solution)/shard_map/ppermute | solution.py:437
  40.8 2.2 %sine_select_fusion.basis = f32[256,512]{1,0:T(8,128)S(1)} fusion(s32[256]{0:T(256)S(1)} %and_select_fusion, pred[256]{0:T(512)(128)(4,1)S(1)} %fusion.7), kind=kLoop, calls=%fused_computation.6 | loop fusion | flops 1966080 | bytes 525568 | tf_op jit(solution)/shard_map/jit(_where)/select_n | solution.py:44
  43.0 3.6 %shard_map.85 = (f32[5,32,256]{2,1,0:T(8,128)S(1)}, f32[5,32,256]{2,1,0:T(8,128)S(1)}, f32[5,32,256]{2,1,0:T(8,128)S(1)}, f32[5,32,256]{2,1,0:T(8,128)S(1)}, f32...) custom-call(f32[3,32,16,256]{3,2,1,0:T(8,128)S(1)} %copy-done, ...), custom_call_target="tpu_custom_call" | custom-call | bytes 7897088 | tf_op jit(solution)/shard_map/pallas_call | solution.py:404
  47.2 2.5 %collective-permute-start.19 = (f32[5,32,256]{2,1,0:T(8,128)S(1)}, f32[5,32,256]{2,1,0:T(8,128)S(1)}, u32[]{:S(2)}, u32[]{:S(2)}) collective-permute-start(f32[5,32,256]{2,1,0:T(8,128)S(1)} %get-tuple-element.80), channel_id=1, source_target_pairs={{0,24},{4,28},{8,16},{12,20},{16,8},{20,12},{24,0},{28,4},{1,25},{... | collective-permute-start | bytes 491528 | tf_op jit(solution)/shard_map/ppermute | solution.py:437
  49.7 2.2 %collective-permute-done.7.refs_5_ = f32[6,32,256]{2,1,0:T(8,128)S(1)} collective-permute-done((f32[6,32,256]{2,1,0:T(8,128)}, f32[6,32,256]{2,1,0:T(8,128)S(1)}, u32[]{:S(2)}, u32[]{:S(2)}) %collective-permute-start.7) | collective-permute-done | bytes 196640 | tf_op jit(solution)/shard_map/ppermute | solution.py:437
  51.9 6.2 %collective-permute-done.8.refs_6_ = f32[6,32,256]{2,1,0:T(8,128)S(1)} collective-permute-done((f32[6,32,256]{2,1,0:T(8,128)}, f32[6,32,256]{2,1,0:T(8,128)S(1)}, u32[]{:S(2)}, u32[]{:S(2)}) %collective-permute-start.8) | collective-permute-done | bytes 196640 | tf_op jit(solution)/shard_map/ppermute | solution.py:437
  58.1 1.9 %copy-done.3 = f32[3,1,2,256,512]{4,3,2,1,0:T(8,128)S(1)} copy-done((f32[3,1,2,256,512]{4,3,2,1,0:T(8,128)S(1)}, f32[3,1,2,256,512]{4,3,2,1,0:T(8,128)}, u32[]{:S(2)}) %copy-start.3) | copy-done | bytes 3145752
  60.0 12.8 %shard_map.86 = (f32[5,32,256]{2,1,0:T(8,128)S(1)}, f32[5,32,256]{2,1,0:T(8,128)S(1)}, f32[5,32,256]{2,1,0:T(8,128)S(1)}, f32[5,32,256]{2,1,0:T(8,128)S(1)}, f32...) custom-call(f32[256,512]{1,0:T(8,128)S(1)} %sine_select_fusion.basis, ...), custom_call_target="tpu_custom_call" | custom-call | flops 2415919104 | bytes 19144704 | tf_op jit(solution)/shard_map/pallas_call | solution.py:404
  74.4 2.5 %collective-permute-start.10 = (f32[5,32,256]{2,1,0:T(8,128)S(1)}, f32[5,32,256]{2,1,0:T(8,128)S(1)}, u32[]{:S(2)}, u32[]{:S(2)}) collective-permute-start(f32[5,32,256]{2,1,0:T(8,128)S(1)} %get-tuple-element.64), channel_id=1, source_target_pairs={{0,24},{4,28},{8,16},{12,20},{16,8},{20,12},{24,0},{28,4},{1,25},{... | collective-permute-start | bytes 491528 | tf_op jit(solution)/shard_map/ppermute | solution.py:437
  78.2 3.8 %collective-permute-start.13 = (f32[5,32,256]{2,1,0:T(8,128)S(1)}, f32[5,32,256]{2,1,0:T(8,128)S(1)}, u32[]{:S(2)}, u32[]{:S(2)}) collective-permute-start(f32[5,32,256]{2,1,0:T(8,128)S(1)} %get-tuple-element.67), channel_id=1, source_target_pairs={{0,16},{4,20},{8,24},{12,28},{16,0},{20,4},{24,8},{28,12},{1,17},{... | collective-permute-start | bytes 491528 | tf_op jit(solution)/shard_map/ppermute | solution.py:437
  82.0 13.5 %collective-permute-start.14 = (f32[5,32,256]{2,1,0:T(8,128)S(1)}, f32[5,32,256]{2,1,0:T(8,128)S(1)}, u32[]{:S(2)}, u32[]{:S(2)}) collective-permute-start(f32[5,32,256]{2,1,0:T(8,128)S(1)} %get-tuple-element.68), channel_id=1, source_target_pairs={{0,12},{4,8},{8,4},{12,0},{16,28},{20,24},{24,20},{28,16},{1,13},{... | collective-permute-start | bytes 491528 | tf_op jit(solution)/shard_map/ppermute | solution.py:437
  95.5 2.6 %collective-permute-start.15 = (f32[5,32,256]{2,1,0:T(8,128)S(1)}, f32[5,32,256]{2,1,0:T(8,128)S(1)}, u32[]{:S(2)}, u32[]{:S(2)}) collective-permute-start(f32[5,32,256]{2,1,0:T(8,128)S(1)} %get-tuple-element.69), channel_id=1, source_target_pairs={{0,8},{4,12},{8,0},{12,4},{16,24},{20,28},{24,16},{28,20},{1,9},{5... | collective-permute-start | bytes 491528 | tf_op jit(solution)/shard_map/ppermute | solution.py:437
  98.1 2.4 %collective-permute-start.20 = (f32[5,32,256]{2,1,0:T(8,128)S(1)}, f32[5,32,256]{2,1,0:T(8,128)S(1)}, u32[]{:S(2)}, u32[]{:S(2)}) collective-permute-start(f32[5,32,256]{2,1,0:T(8,128)S(1)} %get-tuple-element.81), channel_id=1, source_target_pairs={{0,28},{4,24},{8,12},{12,8},{16,20},{20,16},{24,4},{28,0},{1,29},{... | collective-permute-start | bytes 491528 | tf_op jit(solution)/shard_map/ppermute | solution.py:437
  101.4 11.7 %collective-permute-done.13.refs_4_ = f32[5,32,256]{2,1,0:T(8,128)S(1)} collective-permute-done((f32[5,32,256]{2,1,0:T(8,128)S(1)}, f32[5,32,256]{2,1,0:T(8,128)S(1)}, u32[]{:S(2)}, u32[]{:S(2)}) %collective-permute-start.13) | collective-permute-done | bytes 163872 | tf_op jit(solution)/shard_map/ppermute | solution.py:437
  113.1 3.4 %collective-permute-start.23 = (f32[5,32,256]{2,1,0:T(8,128)S(1)}, f32[5,32,256]{2,1,0:T(8,128)S(1)}, u32[]{:S(2)}, u32[]{:S(2)}) collective-permute-start(f32[5,32,256]{2,1,0:T(8,128)S(1)} %get-tuple-element.84), channel_id=1, source_target_pairs={{0,12},{4,8},{8,4},{12,0},{16,28},{20,24},{24,20},{28,16},{1,13},{... | collective-permute-start | bytes 491528 | tf_op jit(solution)/shard_map/ppermute | solution.py:437
  116.5 1.8 %collective-permute-done.15.refs_6_ = f32[5,32,256]{2,1,0:T(8,128)S(1)} collective-permute-done((f32[5,32,256]{2,1,0:T(8,128)S(1)}, f32[5,32,256]{2,1,0:T(8,128)S(1)}, u32[]{:S(2)}, u32[]{:S(2)}) %collective-permute-start.15) | collective-permute-done | bytes 163872 | tf_op jit(solution)/shard_map/ppermute | solution.py:437
  121.1 2.4 %collective-permute-done.23.refs_5_ = f32[5,32,256]{2,1,0:T(8,128)S(1)} collective-permute-done((f32[5,32,256]{2,1,0:T(8,128)S(1)}, f32[5,32,256]{2,1,0:T(8,128)S(1)}, u32[]{:S(2)}, u32[]{:S(2)}) %collective-permute-start.23) | collective-permute-done | bytes 163872 | tf_op jit(solution)/shard_map/ppermute | solution.py:437
  125.3 14.4 %shard_map.89 = (f32[6,32,256]{2,1,0:T(8,128)S(1)}, f32[6,32,256]{2,1,0:T(8,128)S(1)}, f32[6,32,256]{2,1,0:T(8,128)S(1)}, f32[6,32,256]{2,1,0:T(8,128)S(1)}, f32...) custom-call(f32[256,512]{1,0:T(8,128)S(1)} %sine_select_fusion.basis, ...), custom_call_target="tpu_custom_call" | custom-call | flops 2415919104 | bytes 19144704 | tf_op jit(solution)/shard_map/pallas_call | solution.py:404
  140.3 2.5 %collective-permute-start.26 = (f32[6,32,256]{2,1,0:T(8,128)S(1)}, f32[6,32,256]{2,1,0:T(8,128)S(1)}, u32[]{:S(2)}, u32[]{:S(2)}) collective-permute-start(f32[6,32,256]{2,1,0:T(8,128)S(1)} %get-tuple-element.88), channel_id=1, source_target_pairs={{0,24},{4,28},{8,16},{12,20},{16,8},{20,12},{24,0},{28,4},{1,25},{... | collective-permute-start | bytes 589832 | tf_op jit(solution)/shard_map/ppermute | solution.py:437
  144.0 2.3 %collective-permute-start.27 = (f32[6,32,256]{2,1,0:T(8,128)S(1)}, f32[6,32,256]{2,1,0:T(8,128)S(1)}, u32[]{:S(2)}, u32[]{:S(2)}) collective-permute-start(f32[6,32,256]{2,1,0:T(8,128)S(1)} %get-tuple-element.89), channel_id=1, source_target_pairs={{0,28},{4,24},{8,12},{12,8},{16,20},{20,16},{24,4},{28,0},{1,29},{... | collective-permute-start | bytes 589832 | tf_op jit(solution)/shard_map/ppermute | solution.py:437
  146.4 3.4 %collective-permute-start.29 = (f32[6,32,256]{2,1,0:T(8,128)S(1)}, f32[6,32,256]{2,1,0:T(8,128)S(1)}, u32[]{:S(2)}, u32[]{:S(2)}) collective-permute-start(f32[6,32,256]{2,1,0:T(8,128)S(1)} %get-tuple-element.91), channel_id=1, source_target_pairs={{0,16},{4,20},{8,24},{12,28},{16,0},{20,4},{24,8},{28,12},{1,17},{... | collective-permute-start | bytes 589832 | tf_op jit(solution)/shard_map/ppermute | solution.py:437
  149.8 14.1 %collective-permute-start.30 = (f32[6,32,256]{2,1,0:T(8,128)S(1)}, f32[6,32,256]{2,1,0:T(8,128)S(1)}, u32[]{:S(2)}, u32[]{:S(2)}) collective-permute-start(f32[6,32,256]{2,1,0:T(8,128)S(1)} %get-tuple-element.92), channel_id=1, source_target_pairs={{0,12},{4,8},{8,4},{12,0},{16,28},{20,24},{24,20},{28,16},{1,13},{... | collective-permute-start | bytes 589832 | tf_op jit(solution)/shard_map/ppermute | solution.py:437
  163.9 3.1 %collective-permute-start.31 = (f32[6,32,256]{2,1,0:T(8,128)S(1)}, f32[6,32,256]{2,1,0:T(8,128)S(1)}, u32[]{:S(2)}, u32[]{:S(2)}) collective-permute-start(f32[6,32,256]{2,1,0:T(8,128)S(1)} %get-tuple-element.93), channel_id=1, source_target_pairs={{0,8},{4,12},{8,0},{12,4},{16,24},{20,28},{24,16},{28,20},{1,9},{5... | collective-permute-start | bytes 589832 | tf_op jit(solution)/shard_map/ppermute | solution.py:437
  167.0 4.4 %shard_map.88 = (f32[3,16,32,256]{3,2,1,0:T(8,128)S(1)}, f32[3,32,16,256]{3,2,1,0:T(8,128)}) custom-call(f32[3,16,32,256]{3,2,1,0:T(8,128)S(1)} %get-tuple-element.71.e_zk, f32[3,16,32,256]{3,2,1,0:T(8,128)S(1)} %get-tuple-element.53.ahead, f32[3,16,32,256]{3,2,1,0:T(8,128)S(1)} %get-tuple-element.54.h_zk, f32[3,32,256]{2,1,0:T(8,128)S(1)} %collective-permute-done.16.above, ...), custom_call_target="tpu_custom_call" | custom-call | bytes 8159232 | tf_op jit(solution)/shard_map/pallas_call | solution.py:404
  173.3 3.2 %collective-permute-done.30.refs_5_ = f32[6,32,256]{2,1,0:T(8,128)S(1)} collective-permute-done((f32[6,32,256]{2,1,0:T(8,128)S(1)}, f32[6,32,256]{2,1,0:T(8,128)S(1)}, u32[]{:S(2)}, u32[]{:S(2)}) %collective-permute-start.30) | collective-permute-done | bytes 196640 | tf_op jit(solution)/shard_map/ppermute | solution.py:437
  (63 shorter events, 23.0 us)
Async XLA Ops:
  3.4 17.8 %collective-permute-start = (f32[3,32,256]{2,1,0:T(8,128)}, f32[3,32,256]{2,1,0:T(8,128)S(1)}, u32[]{:S(2)}, u32[]{:S(2)}) collective-permute-start(f32[3,32,256]{2,1,0:T(8,128)} %get-tuple-element.51), channel_id=1, source_target_pairs={{1,0},{2,1},{3,2},{5,4},{6,5},{7,6},{9,8},{10,9},{11,10},{13,12},{... | collective-permute-start | bytes 294920 | tf_op jit(solution)/shard_map/ppermute | solution.py:444
  4.7 18.5 %collective-permute-start.1 = (f32[2,3,32,256]{3,2,1,0:T(8,128)}, f32[2,3,32,256]{3,2,1,0:T(8,128)S(1)}, u32[]{:S(2)}, u32[]{:S(2)}) collective-permute-start(f32[2,3,32,256]{3,2,1,0:T(8,128)} %get-tuple-element.52), channel_id=1, source_target_pairs={{0,1},{1,2},{2,3},{4,5},{5,6},{6,7},{8,9},{9,10},{10,11},{12,13},{... | collective-permute-start | bytes 589832 | tf_op jit(solution)/shard_map/ppermute | solution.py:444
  7.7 17.6 %collective-permute-start.2 = (f32[6,32,256]{2,1,0:T(8,128)}, f32[6,32,256]{2,1,0:T(8,128)}, u32[]{:S(2)}, u32[]{:S(2)}) collective-permute-start(f32[6,32,256]{2,1,0:T(8,128)} %get-tuple-element.55), channel_id=1, source_target_pairs={{0,4},{4,0},{8,20},{12,16},{16,12},{20,8},{24,28},{28,24},{1,5},{5... | collective-permute-start | bytes 589832 | tf_op jit(solution)/shard_map/ppermute | solution.py:437
  10.8 26.7 %collective-permute-start.3 = (f32[6,32,256]{2,1,0:T(8,128)}, f32[6,32,256]{2,1,0:T(8,128)}, u32[]{:S(2)}, u32[]{:S(2)}) collective-permute-start(f32[6,32,256]{2,1,0:T(8,128)} %get-tuple-element.56), channel_id=1, source_target_pairs={{0,24},{4,28},{8,16},{12,20},{16,8},{20,12},{24,0},{28,4},{1,25},{... | collective-permute-start | bytes 589832 | tf_op jit(solution)/shard_map/ppermute | solution.py:437
  14.4 32.2 %collective-permute-start.4 = (f32[6,32,256]{2,1,0:T(8,128)}, f32[6,32,256]{2,1,0:T(8,128)}, u32[]{:S(2)}, u32[]{:S(2)}) collective-permute-start(f32[6,32,256]{2,1,0:T(8,128)} %get-tuple-element.57), channel_id=1, source_target_pairs={{0,28},{4,24},{8,12},{12,8},{16,20},{20,16},{24,4},{28,0},{1,29},{... | collective-permute-start | bytes 589832 | tf_op jit(solution)/shard_map/ppermute | solution.py:437
  21.2 26.0 %collective-permute-start.5 = (f32[6,32,256]{2,1,0:T(8,128)}, f32[6,32,256]{2,1,0:T(8,128)S(1)}, u32[]{:S(2)}, u32[]{:S(2)}) collective-permute-start(f32[6,32,256]{2,1,0:T(8,128)} %get-tuple-element.58), channel_id=1, source_target_pairs={{0,20},{4,16},{8,28},{12,24},{16,4},{20,0},{24,12},{28,8},{1,21},{... | collective-permute-start | bytes 589832 | tf_op jit(solution)/shard_map/ppermute | solution.py:437
  23.2 26.5 %collective-permute-start.6 = (f32[6,32,256]{2,1,0:T(8,128)}, f32[6,32,256]{2,1,0:T(8,128)S(1)}, u32[]{:S(2)}, u32[]{:S(2)}) collective-permute-start(f32[6,32,256]{2,1,0:T(8,128)} %get-tuple-element.59), channel_id=1, source_target_pairs={{0,16},{4,20},{8,24},{12,28},{16,0},{20,4},{24,8},{28,12},{1,17},{... | collective-permute-start | bytes 589832 | tf_op jit(solution)/shard_map/ppermute | solution.py:437
  25.3 26.6 %collective-permute-start.7 = (f32[6,32,256]{2,1,0:T(8,128)}, f32[6,32,256]{2,1,0:T(8,128)S(1)}, u32[]{:S(2)}, u32[]{:S(2)}) collective-permute-start(f32[6,32,256]{2,1,0:T(8,128)} %get-tuple-element.60), channel_id=1, source_target_pairs={{0,12},{4,8},{8,4},{12,0},{16,28},{20,24},{24,20},{28,16},{1,13},{... | collective-permute-start | bytes 589832 | tf_op jit(solution)/shard_map/ppermute | solution.py:437
  37.5 20.6 %collective-permute-start.8 = (f32[6,32,256]{2,1,0:T(8,128)}, f32[6,32,256]{2,1,0:T(8,128)S(1)}, u32[]{:S(2)}, u32[]{:S(2)}) collective-permute-start(f32[6,32,256]{2,1,0:T(8,128)} %get-tuple-element.61), channel_id=1, source_target_pairs={{0,8},{4,12},{8,0},{12,4},{16,24},{20,28},{24,16},{28,20},{1,9},{5... | collective-permute-start | bytes 589832 | tf_op jit(solution)/shard_map/ppermute | solution.py:437
  46.6 31.6 %collective-permute-start.18 = (f32[5,32,256]{2,1,0:T(8,128)S(1)}, f32[5,32,256]{2,1,0:T(8,128)S(1)}, u32[]{:S(2)}, u32[]{:S(2)}) collective-permute-start(f32[5,32,256]{2,1,0:T(8,128)S(1)} %get-tuple-element.79), channel_id=1, source_target_pairs={{0,4},{4,0},{8,20},{12,16},{16,12},{20,8},{24,28},{28,24},{1,5},{5... | collective-permute-start | bytes 491528 | tf_op jit(solution)/shard_map/ppermute | solution.py:437
  47.2 31.0 %collective-permute-start.19 = (f32[5,32,256]{2,1,0:T(8,128)S(1)}, f32[5,32,256]{2,1,0:T(8,128)S(1)}, u32[]{:S(2)}, u32[]{:S(2)}) collective-permute-start(f32[5,32,256]{2,1,0:T(8,128)S(1)} %get-tuple-element.80), channel_id=1, source_target_pairs={{0,24},{4,28},{8,16},{12,20},{16,8},{20,12},{24,0},{28,4},{1,25},{... | collective-permute-start | bytes 491528 | tf_op jit(solution)/shard_map/ppermute | solution.py:437
  72.8 9.2 %collective-permute-start.9 = (f32[5,32,256]{2,1,0:T(8,128)S(1)}, f32[5,32,256]{2,1,0:T(8,128)S(1)}, u32[]{:S(2)}, u32[]{:S(2)}) collective-permute-start(f32[5,32,256]{2,1,0:T(8,128)S(1)} %get-tuple-element.63), channel_id=1, source_target_pairs={{0,4},{4,0},{8,20},{12,16},{16,12},{20,8},{24,28},{28,24},{1,5},{5... | collective-permute-start | bytes 491528 | tf_op jit(solution)/shard_map/ppermute | solution.py:437
  74.4 21.2 %collective-permute-start.10 = (f32[5,32,256]{2,1,0:T(8,128)S(1)}, f32[5,32,256]{2,1,0:T(8,128)S(1)}, u32[]{:S(2)}, u32[]{:S(2)}) collective-permute-start(f32[5,32,256]{2,1,0:T(8,128)S(1)} %get-tuple-element.64), channel_id=1, source_target_pairs={{0,24},{4,28},{8,16},{12,20},{16,8},{20,12},{24,0},{28,4},{1,25},{... | collective-permute-start | bytes 491528 | tf_op jit(solution)/shard_map/ppermute | solution.py:437
  76.9 21.2 %collective-permute-start.11 = (f32[5,32,256]{2,1,0:T(8,128)S(1)}, f32[5,32,256]{2,1,0:T(8,128)S(1)}, u32[]{:S(2)}, u32[]{:S(2)}) collective-permute-start(f32[5,32,256]{2,1,0:T(8,128)S(1)} %get-tuple-element.65), channel_id=1, source_target_pairs={{0,28},{4,24},{8,12},{12,8},{16,20},{20,16},{24,4},{28,0},{1,29},{... | collective-permute-start | bytes 491528 | tf_op jit(solution)/shard_map/ppermute | solution.py:437
  78.2 23.2 %collective-permute-start.12 = (f32[5,32,256]{2,1,0:T(8,128)S(1)}, f32[5,32,256]{2,1,0:T(8,128)S(1)}, u32[]{:S(2)}, u32[]{:S(2)}) collective-permute-start(f32[5,32,256]{2,1,0:T(8,128)S(1)} %get-tuple-element.66), channel_id=1, source_target_pairs={{0,20},{4,16},{8,28},{12,24},{16,4},{20,0},{24,12},{28,8},{1,21},{... | collective-permute-start | bytes 491528 | tf_op jit(solution)/shard_map/ppermute | solution.py:437
  78.2 34.9 %collective-permute-start.13 = (f32[5,32,256]{2,1,0:T(8,128)S(1)}, f32[5,32,256]{2,1,0:T(8,128)S(1)}, u32[]{:S(2)}, u32[]{:S(2)}) collective-permute-start(f32[5,32,256]{2,1,0:T(8,128)S(1)} %get-tuple-element.67), channel_id=1, source_target_pairs={{0,16},{4,20},{8,24},{12,28},{16,0},{20,4},{24,8},{28,12},{1,17},{... | collective-permute-start | bytes 491528 | tf_op jit(solution)/shard_map/ppermute | solution.py:437
  82.0 31.1 %collective-permute-start.14 = (f32[5,32,256]{2,1,0:T(8,128)S(1)}, f32[5,32,256]{2,1,0:T(8,128)S(1)}, u32[]{:S(2)}, u32[]{:S(2)}) collective-permute-start(f32[5,32,256]{2,1,0:T(8,128)S(1)} %get-tuple-element.68), channel_id=1, source_target_pairs={{0,12},{4,8},{8,4},{12,0},{16,28},{20,24},{24,20},{28,16},{1,13},{... | collective-permute-start | bytes 491528 | tf_op jit(solution)/shard_map/ppermute | solution.py:437
  95.5 22.8 %collective-permute-start.15 = (f32[5,32,256]{2,1,0:T(8,128)S(1)}, f32[5,32,256]{2,1,0:T(8,128)S(1)}, u32[]{:S(2)}, u32[]{:S(2)}) collective-permute-start(f32[5,32,256]{2,1,0:T(8,128)S(1)} %get-tuple-element.69), channel_id=1, source_target_pairs={{0,8},{4,12},{8,0},{12,4},{16,24},{20,28},{24,16},{28,20},{1,9},{5... | collective-permute-start | bytes 491528 | tf_op jit(solution)/shard_map/ppermute | solution.py:437
  98.1 20.4 %collective-permute-start.20 = (f32[5,32,256]{2,1,0:T(8,128)S(1)}, f32[5,32,256]{2,1,0:T(8,128)S(1)}, u32[]{:S(2)}, u32[]{:S(2)}) collective-permute-start(f32[5,32,256]{2,1,0:T(8,128)S(1)} %get-tuple-element.81), channel_id=1, source_target_pairs={{0,28},{4,24},{8,12},{12,8},{16,20},{20,16},{24,4},{28,0},{1,29},{... | collective-permute-start | bytes 491528 | tf_op jit(solution)/shard_map/ppermute | solution.py:437
  101.4 18.4 %collective-permute-start.21 = (f32[5,32,256]{2,1,0:T(8,128)S(1)}, f32[5,32,256]{2,1,0:T(8,128)S(1)}, u32[]{:S(2)}, u32[]{:S(2)}) collective-permute-start(f32[5,32,256]{2,1,0:T(8,128)S(1)} %get-tuple-element.82), channel_id=1, source_target_pairs={{0,20},{4,16},{8,28},{12,24},{16,4},{20,0},{24,12},{28,8},{1,21},{... | collective-permute-start | bytes 491528 | tf_op jit(solution)/shard_map/ppermute | solution.py:437
  113.1 8.0 %collective-permute-start.22 = (f32[5,32,256]{2,1,0:T(8,128)S(1)}, f32[5,32,256]{2,1,0:T(8,128)S(1)}, u32[]{:S(2)}, u32[]{:S(2)}) collective-permute-start(f32[5,32,256]{2,1,0:T(8,128)S(1)} %get-tuple-element.83), channel_id=1, source_target_pairs={{0,16},{4,20},{8,24},{12,28},{16,0},{20,4},{24,8},{28,12},{1,17},{... | collective-permute-start | bytes 491528 | tf_op jit(solution)/shard_map/ppermute | solution.py:437
  113.1 10.4 %collective-permute-start.23 = (f32[5,32,256]{2,1,0:T(8,128)S(1)}, f32[5,32,256]{2,1,0:T(8,128)S(1)}, u32[]{:S(2)}, u32[]{:S(2)}) collective-permute-start(f32[5,32,256]{2,1,0:T(8,128)S(1)} %get-tuple-element.84), channel_id=1, source_target_pairs={{0,12},{4,8},{8,4},{12,0},{16,28},{20,24},{24,20},{28,16},{1,13},{... | collective-permute-start | bytes 491528 | tf_op jit(solution)/shard_map/ppermute | solution.py:437
  118.3 7.0 %collective-permute-start.24 = (f32[5,32,256]{2,1,0:T(8,128)S(1)}, f32[5,32,256]{2,1,0:T(8,128)S(1)}, u32[]{:S(2)}, u32[]{:S(2)}) collective-permute-start(f32[5,32,256]{2,1,0:T(8,128)S(1)} %get-tuple-element.85), channel_id=1, source_target_pairs={{0,8},{4,12},{8,0},{12,4},{16,24},{20,28},{24,16},{28,20},{1,9},{5... | collective-permute-start | bytes 491528 | tf_op jit(solution)/shard_map/ppermute | solution.py:437
  118.5 27.9 %collective-permute-start.17 = (f32[2,3,32,256]{3,2,1,0:T(8,128)S(1)}, f32[2,3,32,256]{3,2,1,0:T(8,128)S(1)}, u32[]{:S(2)}, u32[]{:S(2)}) collective-permute-start(f32[2,3,32,256]{3,2,1,0:T(8,128)S(1)} %get-tuple-element.73), channel_id=1, source_target_pairs={{0,1},{1,2},{2,3},{4,5},{5,6},{6,7},{8,9},{9,10},{10,11},{12,13},{... | collective-permute-start | bytes 589832 | tf_op jit(solution)/shard_map/ppermute | solution.py:444
  139.7 10.0 %collective-permute-start.25 = (f32[6,32,256]{2,1,0:T(8,128)S(1)}, f32[6,32,256]{2,1,0:T(8,128)S(1)}, u32[]{:S(2)}, u32[]{:S(2)}) collective-permute-start(f32[6,32,256]{2,1,0:T(8,128)S(1)} %get-tuple-element.87), channel_id=1, source_target_pairs={{0,4},{4,0},{8,20},{12,16},{16,12},{20,8},{24,28},{28,24},{1,5},{5... | collective-permute-start | bytes 589832 | tf_op jit(solution)/shard_map/ppermute | solution.py:437
  140.3 23.6 %collective-permute-start.26 = (f32[6,32,256]{2,1,0:T(8,128)S(1)}, f32[6,32,256]{2,1,0:T(8,128)S(1)}, u32[]{:S(2)}, u32[]{:S(2)}) collective-permute-start(f32[6,32,256]{2,1,0:T(8,128)S(1)} %get-tuple-element.88), channel_id=1, source_target_pairs={{0,24},{4,28},{8,16},{12,20},{16,8},{20,12},{24,0},{28,4},{1,25},{... | collective-permute-start | bytes 589832 | tf_op jit(solution)/shard_map/ppermute | solution.py:437
  142.7 3.6 %collective-permute-start.16 = (f32[3,32,256]{2,1,0:T(8,128)S(1)}, f32[3,32,256]{2,1,0:T(8,128)S(1)}, u32[]{:S(2)}, u32[]{:S(2)}) collective-permute-start(f32[3,32,256]{2,1,0:T(8,128)S(1)} %get-tuple-element.72), channel_id=1, source_target_pairs={{1,0},{2,1},{3,2},{5,4},{6,5},{7,6},{9,8},{10,9},{11,10},{13,12},{... | collective-permute-start | bytes 294920 | tf_op jit(solution)/shard_map/ppermute | solution.py:444
  144.0 27.3 %collective-permute-start.27 = (f32[6,32,256]{2,1,0:T(8,128)S(1)}, f32[6,32,256]{2,1,0:T(8,128)S(1)}, u32[]{:S(2)}, u32[]{:S(2)}) collective-permute-start(f32[6,32,256]{2,1,0:T(8,128)S(1)} %get-tuple-element.89), channel_id=1, source_target_pairs={{0,28},{4,24},{8,12},{12,8},{16,20},{20,16},{24,4},{28,0},{1,29},{... | collective-permute-start | bytes 589832 | tf_op jit(solution)/shard_map/ppermute | solution.py:437
  146.4 25.9 %collective-permute-start.28 = (f32[6,32,256]{2,1,0:T(8,128)S(1)}, f32[6,32,256]{2,1,0:T(8,128)S(1)}, u32[]{:S(2)}, u32[]{:S(2)}) collective-permute-start(f32[6,32,256]{2,1,0:T(8,128)S(1)} %get-tuple-element.90), channel_id=1, source_target_pairs={{0,20},{4,16},{8,28},{12,24},{16,4},{20,0},{24,12},{28,8},{1,21},{... | collective-permute-start | bytes 589832 | tf_op jit(solution)/shard_map/ppermute | solution.py:437
  146.4 26.9 %collective-permute-start.29 = (f32[6,32,256]{2,1,0:T(8,128)S(1)}, f32[6,32,256]{2,1,0:T(8,128)S(1)}, u32[]{:S(2)}, u32[]{:S(2)}) collective-permute-start(f32[6,32,256]{2,1,0:T(8,128)S(1)} %get-tuple-element.91), channel_id=1, source_target_pairs={{0,16},{4,20},{8,24},{12,28},{16,0},{20,4},{24,8},{28,12},{1,17},{... | collective-permute-start | bytes 589832 | tf_op jit(solution)/shard_map/ppermute | solution.py:437
  149.8 26.8 %collective-permute-start.30 = (f32[6,32,256]{2,1,0:T(8,128)S(1)}, f32[6,32,256]{2,1,0:T(8,128)S(1)}, u32[]{:S(2)}, u32[]{:S(2)}) collective-permute-start(f32[6,32,256]{2,1,0:T(8,128)S(1)} %get-tuple-element.92), channel_id=1, source_target_pairs={{0,12},{4,8},{8,4},{12,0},{16,28},{20,24},{24,20},{28,16},{1,13},{... | collective-permute-start | bytes 589832 | tf_op jit(solution)/shard_map/ppermute | solution.py:437
  163.9 13.5 %collective-permute-start.31 = (f32[6,32,256]{2,1,0:T(8,128)S(1)}, f32[6,32,256]{2,1,0:T(8,128)S(1)}, u32[]{:S(2)}, u32[]{:S(2)}) collective-permute-start(f32[6,32,256]{2,1,0:T(8,128)S(1)} %get-tuple-element.93), channel_id=1, source_target_pairs={{0,8},{4,12},{8,0},{12,4},{16,24},{20,28},{24,16},{28,20},{1,9},{5... | collective-permute-start | bytes 589832 | tf_op jit(solution)/shard_map/ppermute | solution.py:437
  (6 other events, 97.9 us)
where the time goes:
time: 179 us
  starting transfers between devices  93.2 us (52%)
  Pallas kernels  39.4 us (22%)
  waiting for transfers between devices  34.4 us (19%)
  local copies, waits for them, and re-layouts  6.21 us (3%)
  other arithmetic  4.63 us (3%)
    ppermute x28, starting transfers between devices, exchange(): moved.append(lax.ppermute(blocks[s], 'mode', pairs))  86.3 us
    pallas_call x7, Pallas kernels, call(): pl.pallas_call(kernel, out_shape=out, in_specs=[pl.BlockSpec(memory_space...  39.4 us
    ppermute x28, waiting for transfers between devices, exchange(): moved.append(lax.ppermute(blocks[s], 'mode', pairs))  34.4 us
    ppermute x4, starting transfers between devices, along(): lax.ppermute(value, 'gz', [(i, i + steps) for i in range(first, last)])  6.91 us
  transfers between devices with their start and end apart: 32, of which 12 were waited for; matrix products, arithmetic and copies ran while one was open for 5% of the time, Pallas kernels for 20%

commit v1 on v0

--- a/solution.py
+++ b/solution.py
@@ -10,17 +10,28 @@
 
 
 SUBSTEPS = 4
-LANES = 128
+LANES = 256
 RATIO = 0.5
 
 
 def distances(peers):
     quarter = peers // 4
-    far, near = list(range(3 * quarter, peers)), list(range(1, quarter))
-    middle = list(range(3 * quarter - 1, quarter - 1, -1))
-    far.reverse()
-    inner, outer = far[:1] + far[1:] + near, near[:1] + far[1:] + far[:1] + near[1:]
+    far, near = list(range(peers - 1, 3 * quarter - 1, -1)), list(range(1, quarter))
+    middle = [s + odd for s in range(3 * quarter - 2, quarter - 1, -2) for odd in (0, 1)]
+    inner, outer = far + near, near[:1] + far[1:] + far[:1] + near[1:]
     return inner + middle + [0], outer + middle + [0]
+
+
+def is_even(s, peers):
+    return distances(peers)[0][s] % 2 == 0
+
+
+def evens(blocks):
+    return [block for s, block in enumerate(blocks) if is_even(s, len(blocks))]
+
+
+def of_pair(index, modes):
+    return pl.ds(pl.multiple_of((index >> 1) * modes, modes), modes)
 
 
 def peer(me, s, peers):
@@ -75,6 +86,10 @@
 
     def up(self, x):
         return jnp.where(self.lane == self.radii - 1, 0.0, pltpu.roll(x, self.radii - 1, 1)) - x
+
+    def flux(self, radial, azimuth):
+        spread = self.up(self.inner * radial) + self.rotate(azimuth)
+        return (self.time_step / RATIO) * self.per_outer * spread
 
     def magnetic(self, e, e_above, h):
         ts = self.time_step
@@ -159,9 +174,13 @@
         for c in range(2):
             for q in range(planes):
                 e_zk[c, first + q] = ahead[c, first + q] - blocks[s][c * planes + q]
-        for q in range(planes - 1):
+        for q in range(planes):
             e_zk[2, first + q] = ahead[2, first + q]
-        e_zk[2, first + planes - 1] = ahead[2, first + planes - 1] - blocks[s][2 * planes]
+    for s in range(peers):
+        if is_even(s, peers):
+            index = peer(me, s, peers)
+            at = (index - (index & 1)) * planes + planes - 1
+            e_zk[2, at] = ahead[2, at] - blocks[s][2 * planes]
     for c in range(3):
         to_lower[c] = e_zk[c, 0]
         to_upper[0, c] = e_zk[c, last]
@@ -222,7 +241,8 @@
         for c in range(2):
             for q in range(planes):
                 blocks[s][c * planes + q] = curl[c, first + q]
-        blocks[s][2 * planes] = curl[2, first]
+        if is_even(s, peers):
+            blocks[s][2 * planes] = curl[2, first + (me & 1) * (planes - 1)]
 
 
 def last_kernel(peers, e_zk, ahead, h_zk, above, below, ahead_new, h_kz, h_new):
@@ -286,7 +306,7 @@
                 points[c, at, part] = p[c] - before[c]
         return carry
 
-    lax.fori_loop(0, rows // 8, loop, 0, unroll=2)
+    lax.fori_loop(0, rows // 8, loop, 0, unroll=4)
     modes = high.shape[0]
     weight = jnp.where(
         lax.broadcasted_iota(jnp.int32, (modes, rows), 0) == 0, 1.0 / angles, 2.0 / angles
@@ -326,7 +346,7 @@
 def gas_first_kernel(peers, planes, basis, coefficient, polar, velocity, *refs):
     arrived, refs = refs[:peers], refs[peers:]
     blocks, refs = refs[:peers], refs[peers:]
-    new_polar, new_velocity, change, rest, fields, points, high, low = refs
+    new_polar, new_velocity, change, rest, message, fields, points, high, low = refs
     me = lax.axis_index("mode")
     modes, radii = arrived[0].shape[1:]
 
@@ -339,25 +359,52 @@
     gas_step(fields, points, high, low, polar, velocity, coefficient, new_polar, new_velocity, change)
 
     for s in range(peers):
-        first = peer(me, s, peers) * modes
-        at = pl.ds(pl.multiple_of(first, modes), modes)
-        op = Plane(first, modes, radii, modes * peers)
+        index = peer(me, s, peers)
+        at = pl.ds(pl.multiple_of(index * modes, modes), modes)
+        op = Plane(index * modes, modes, radii, modes * peers)
         for n in range(3 * planes):
             rest[n, at, :] = fields[n, at, :] - change[n, at, :]
-        phi, axial = None, change[2 * planes, at, :]
+        total = change[2 * planes, at, :]
+        for q in range(1, planes):
+            total = total + change[2 * planes + q, at, :]
+        if is_even(s, peers):
+            blocks[s][2 * planes] = total
+        else:
+            message[of_pair(index, modes)] = total
+        below = jnp.where(me % 2 == 1, total, 0.0)
         for q in range(planes):
-            for c in range(2):
-                sent = change[c * planes + q, at, :]
-                if phi is not None:
-                    sent = sent + (op.down(phi) if c == 0 else op.per_outer * op.rotate(phi))
-                blocks[s][c * planes + q] = sent
-            if q < planes - 1:
-                phi = (-op.time_step / RATIO) * axial
-                axial = axial + change[2 * planes + q + 1, at, :]
-        blocks[s][2 * planes] = axial
-
-
-def gas_last_kernel(peers, planes, basis, coefficient, polar, velocity, rest, earlier, *refs):
+            phi = (op.time_step / RATIO) * below
+            blocks[s][q] = change[q, at, :] + op.down(phi)
+            blocks[s][planes + q] = change[planes + q, at, :] + op.per_outer * op.rotate(phi)
+            below = below - change[2 * planes + q, at, :]
+
+
+def seal_kernel(peers, message, *refs):
+    blocks, sealed = refs[: len(refs) // 2], refs[len(refs) // 2 :]
+    me = lax.axis_index("mode")
+    where = [s for s in range(peers) if is_even(s, peers)]
+    for s, block, out in zip(where, blocks, sealed):
+        count, modes, _ = block.shape
+        for n in range(count - 1):
+            out[n] = block[n]
+        out[count - 1] = block[count - 1] + message[of_pair(peer(me, s, peers), modes)]
+
+
+def recover_kernel(peers, *refs):
+    blocks, message = refs[:-1], refs[-1]
+    me = lax.axis_index("mode")
+    where = [s for s in range(peers) if is_even(s, peers)]
+    for s, block in zip(where, blocks):
+        count, modes, radii = block.shape
+        planes = count // 2
+        index = peer(me, s, peers)
+        op = Plane(index * modes, modes, radii, modes * peers)
+        flux = [op.flux(block[q], block[planes + q]) for q in range(planes)]
+        first = block[2 * planes]
+        message[of_pair(index, modes)] = jnp.where(me % 2 == 1, first + sum(flux), first - sum(flux[1:]))
+
+
+def gas_last_kernel(peers, planes, basis, coefficient, polar, velocity, rest, earlier, message, *refs):
     arrived, refs = refs[:peers], refs[peers:]
     blocks, refs = refs[:peers], refs[peers:]
     new_polar, new_velocity, fields, points, change, high, low = refs
@@ -366,16 +413,20 @@
 
     high[...], low[...] = split(basis[...])
     for s in range(peers):
-        first = peer(me, s, peers) * modes
-        at = pl.ds(pl.multiple_of(first, modes), modes)
-        op = Plane(first, modes, radii, modes * peers)
-        axial = arrived[s][2 * planes]
+        index = peer(me, s, peers)
+        at = pl.ds(pl.multiple_of(index * modes, modes), modes)
+        op = Plane(index * modes, modes, radii, modes * peers)
+        flux = [op.flux(arrived[s][q], arrived[s][planes + q]) for q in range(planes)]
+        if is_even(s, peers):
+            known = arrived[s][2 * planes]
+            axial = known + jnp.where(me % 2 == 1, sum(flux[1:]), 0.0)
+        else:
+            known = message[of_pair(index, modes)]
+            axial = known + jnp.where(me % 2 == 1, -flux[0], sum(flux[1:]))
         for q in range(planes):
-            radial, azimuth = arrived[s][q], arrived[s][planes + q]
             if q > 0:
-                flux = op.up(op.inner * radial) + op.rotate(azimuth)
-                axial = axial - (op.time_step / RATIO) * op.per_outer * flux
-            for c, found in enumerate((radial, azimuth, axial)):
+                axial = axial - flux[q]
+            for c, found in enumerate((arrived[s][q], arrived[s][planes + q], axial)):
                 n = c * planes + q
                 fields[n, at, :] = rest[n, at, :] + found
 
@@ -444,13 +495,18 @@
     return lax.ppermute(value, "gz", [(i, i + steps) for i in range(first, last)])
 
 
+def swap(value):
+    return lax.ppermute(value, "mode", [(i, i ^ 1) for i in range(lax.axis_size("mode"))])
+
+
 def run(efield, hfield, polar, velocity, material):
     peers = lax.axis_size("mode")
     _, modes, depth, radii = efield.shape
     planes = depth // peers
     angles = polar.shape[4]
     electric = [f32(3 * planes, modes, radii)] * peers
-    curled = [f32(2 * planes + 1, modes, radii)] * peers
+    curled = [f32(2 * planes + is_even(s, peers), modes, radii) for s in range(peers)]
+    half = f32(modes * peers // 2, radii)
     zk = f32(3, depth, modes, radii)
     kz = f32(3, modes, depth, radii)
     lower, upper = f32(3, modes, radii), f32(2, 3, modes, radii)
@@ -477,14 +533,18 @@
     curl_arrived = exchange(curl_blocks)
 
     held = f32(3 * planes, modes * peers, radii)
-    *back, polar, velocity, change, rest = gas_call(
+    *back, polar, velocity, change, rest, sums = gas_call(
         gas_first_kernel, basis, coefficient, polar, velocity,
-        [], arrived, curled, [held, held], planes,
-    )
+        [], arrived, curled, [held, held, half], planes,
+    )
+    sealed = iter(call(functools.partial(seal_kernel, peers), evens(curled), swap(sums), *evens(back)))
+    back = [next(sealed) if is_even(s, peers) else block for s, block in enumerate(back)]
     returned = exchange(back)
+    (axial,) = call(functools.partial(recover_kernel, peers), [half], *evens(curl_arrived))
+    axial = swap(axial)
     *back, polar, velocity = gas_call(
         gas_last_kernel, basis, coefficient, polar, velocity,
-        [rest, change], curl_arrived, electric, [], planes,
+        [rest, change, axial], curl_arrived, electric, [], planes,
     )
     total = exchange(back)
 

time: 179 us -> 185 us (1.034)
  waiting for transfers between devices: 34.4 us -> 44.7 us
  Pallas kernels: 39.4 us -> 35.4 us
    ppermute x28, waiting for transfers between devices: 34.4 us -> 40.1 us  [exchange(): moved.append(lax.ppermute(blocks[s], 'mode', pairs))]
    pallas_call x7 -> x9, Pallas kernels: 39.4 us -> 35.4 us  [call(): pl.pallas_call(kernel, out_shape=out, in_specs=[pl.BlockSpec(memory_space...]
    ppermute x0 -> x2, waiting for transfers between devices: none -> 2.71 us  [swap(): lax.ppermute(value, 'mode', [(i, i ^ 1) for i in range(lax.axis_size('mod...]
    ppermute x0 -> x2, starting transfers between devices: none -> 2.09 us  [swap(): lax.ppermute(value, 'mode', [(i, i ^ 1) for i in range(lax.axis_size('mod...]
    ppermute x4, waiting for transfers between devices: 0.01 us -> 1.95 us  [along(): lax.ppermute(value, 'gz', [(i, i + steps) for i in range(first, last)])]
  transfers between devices with their start and end apart: 32 -> 34, of which waited for: 12 -> 14; matrix products, arithmetic and copies ran while one was open for 5% -> 5% of each run, Pallas kernels for 20% -> 17%
where the time goes in v1:
time: 185 us
  starting transfers between devices  93 us (50%)
  waiting for transfers between devices  44.7 us (24%)
  Pallas kernels  35.4 us (19%)
  local copies, waits for them, and re-layouts  6.21 us (3%)
  other arithmetic  4.64 us (3%)
    ppermute x28, starting transfers between devices, exchange(): moved.append(lax.ppermute(blocks[s], 'mode', pairs))  85.6 us
    ppermute x28, waiting for transfers between devices, exchange(): moved.append(lax.ppermute(blocks[s], 'mode', pairs))  40.1 us
    pallas_call x9, Pallas kernels, call(): pl.pallas_call(kernel, out_shape=out, in_specs=[pl.BlockSpec(memory_space...  35.4 us
    ppermute x4, starting transfers between devices, along(): lax.ppermute(value, 'gz', [(i, i + steps) for i in range(first, last)])  5.34 us
  transfers between devices with their start and end apart: 34, of which 14 were waited for; matrix products, arithmetic and copies ran while one was open for 5% of the time, Pallas kernels for 17%

profile of v1, /device:TPU:0, one launch (start us, length us, event | category | flops | bytes accessed | tf_op | source)
XLA Modules:
  0.0 185.0 jit_solution(12190103979084151016)
XLA Ops:
  0.6 2.7 %shard_map.84 = (f32[6,32,256]{2,1,0:T(8,128)}, f32[6,32,256]{2,1,0:T(8,128)}, f32[6,32,256]{2,1,0:T(8,128)}, f32[6,32,256]{2,1,0:T(8,128)}, f32[6,32,256]{2,1,0...) custom-call(f32[3,32,16,256]{3,2,1,0:T(8,128)} %e_kz.3, ...), custom_call_target="tpu_custom_call" | custom-call | bytes 5013504 | tf_op jit(solution)/shard_map/pallas_call | solution.py:455
  3.4 3.1 %collective-permute-start.2 = (f32[6,32,256]{2,1,0:T(8,128)}, f32[6,32,256]{2,1,0:T(8,128)S(1)}, u32[]{:S(2)}, u32[]{:S(2)}) collective-permute-start(f32[6,32,256]{2,1,0:T(8,128)} %get-tuple-element.60), channel_id=1, source_target_pairs={{0,4},{4,0},{8,20},{12,16},{16,12},{20,8},{24,28},{28,24},{1,5},{5... | collective-permute-start | bytes 589832 | tf_op jit(solution)/shard_map/ppermute | solution.py:488
  6.4 3.6 %collective-permute-start.3 = (f32[6,32,256]{2,1,0:T(8,128)}, f32[6,32,256]{2,1,0:T(8,128)}, u32[]{:S(2)}, u32[]{:S(2)}) collective-permute-start(f32[6,32,256]{2,1,0:T(8,128)} %get-tuple-element.61), channel_id=1, source_target_pairs={{0,24},{4,28},{8,16},{12,20},{16,8},{20,12},{24,0},{28,4},{1,25},{... | collective-permute-start | bytes 589832 | tf_op jit(solution)/shard_map/ppermute | solution.py:488
  11.0 3.1 %collective-permute-start.6 = (f32[6,32,256]{2,1,0:T(8,128)}, f32[6,32,256]{2,1,0:T(8,128)}, u32[]{:S(2)}, u32[]{:S(2)}) collective-permute-start(f32[6,32,256]{2,1,0:T(8,128)} %get-tuple-element.64), channel_id=1, source_target_pairs={{0,20},{4,16},{8,28},{12,24},{16,4},{20,0},{24,12},{28,8},{1,21},{... | collective-permute-start | bytes 589832 | tf_op jit(solution)/shard_map/ppermute | solution.py:488
  20.9 11.3 %collective-permute-start.7 = (f32[6,32,256]{2,1,0:T(8,128)}, f32[6,32,256]{2,1,0:T(8,128)S(1)}, u32[]{:S(2)}, u32[]{:S(2)}) collective-permute-start(f32[6,32,256]{2,1,0:T(8,128)} %get-tuple-element.65), channel_id=1, source_target_pairs={{0,8},{4,12},{8,0},{12,4},{16,24},{20,28},{24,16},{28,20},{1,9},{5... | collective-permute-start | bytes 589832 | tf_op jit(solution)/shard_map/ppermute | solution.py:488
  32.2 4.3 %collective-permute-start.8 = (f32[6,32,256]{2,1,0:T(8,128)}, f32[6,32,256]{2,1,0:T(8,128)S(1)}, u32[]{:S(2)}, u32[]{:S(2)}) collective-permute-start(f32[6,32,256]{2,1,0:T(8,128)} %get-tuple-element.66), channel_id=1, source_target_pairs={{0,12},{4,8},{8,4},{12,0},{16,28},{20,24},{24,20},{28,16},{1,13},{... | collective-permute-start | bytes 589832 | tf_op jit(solution)/shard_map/ppermute | solution.py:488
  36.5 2.2 %sine_select_fusion.basis = f32[256,512]{1,0:T(8,128)S(1)} fusion(s32[256]{0:T(256)S(1)} %and_select_fusion, pred[256]{0:T(512)(128)(4,1)S(1)} %fusion.7), kind=kLoop, calls=%fused_computation.6 | loop fusion | flops 1966080 | bytes 525568 | tf_op jit(solution)/shard_map/jit(_where)/select_n | solution.py:55
  40.3 3.0 %collective-permute-done.6.refs_4_ = f32[6,32,256]{2,1,0:T(8,128)} collective-permute-done((f32[6,32,256]{2,1,0:T(8,128)}, f32[6,32,256]{2,1,0:T(8,128)}, u32[]{:S(2)}, u32[]{:S(2)}) %collective-permute-start.6) | collective-permute-done | bytes 196640 | tf_op jit(solution)/shard_map/ppermute | solution.py:488
  43.4 2.3 %collective-permute-done.7.refs_5_ = f32[6,32,256]{2,1,0:T(8,128)S(1)} collective-permute-done((f32[6,32,256]{2,1,0:T(8,128)}, f32[6,32,256]{2,1,0:T(8,128)S(1)}, u32[]{:S(2)}, u32[]{:S(2)}) %collective-permute-start.7) | collective-permute-done | bytes 196640 | tf_op jit(solution)/shard_map/ppermute | solution.py:488
  45.7 3.3 %collective-permute-done.8.refs_6_ = f32[6,32,256]{2,1,0:T(8,128)S(1)} collective-permute-done((f32[6,32,256]{2,1,0:T(8,128)}, f32[6,32,256]{2,1,0:T(8,128)S(1)}, u32[]{:S(2)}, u32[]{:S(2)}) %collective-permute-start.8) | collective-permute-done | bytes 196640 | tf_op jit(solution)/shard_map/ppermute | solution.py:488
  50.9 10.8 %shard_map.86 = (f32[4,32,256]{2,1,0:T(8,128)S(1)}, f32[5,32,256]{2,1,0:T(8,128)S(1)}, f32[4,32,256]{2,1,0:T(8,128)S(1)}, f32[5,32,256]{2,1,0:T(8,128)S(1)}, f32...) custom-call(f32[256,512]{1,0:T(8,128)S(1)} %sine_select_fusion.basis, ...), custom_call_target="tpu_custom_call" | custom-call | flops 2415919104 | bytes 19144704 | tf_op jit(solution)/shard_map/pallas_call | solution.py:455
  66.0 3.6 %shard_map.85 = (f32[4,32,256]{2,1,0:T(8,128)S(1)}, f32[5,32,256]{2,1,0:T(8,128)S(1)}, f32[4,32,256]{2,1,0:T(8,128)S(1)}, f32[5,32,256]{2,1,0:T(8,128)S(1)}, f32...) custom-call(f32[3,32,16,256]{3,2,1,0:T(8,128)S(1)} %copy-done, ...), custom_call_target="tpu_custom_call" | custom-call | bytes 7766016 | tf_op jit(solution)/shard_map/pallas_call | solution.py:455
  69.6 2.6 %collective-permute-start.19 = (f32[5,32,256]{2,1,0:T(8,128)S(1)}, f32[5,32,256]{2,1,0:T(8,128)S(1)}, u32[]{:S(2)}, u32[]{:S(2)}) collective-permute-start(f32[5,32,256]{2,1,0:T(8,128)S(1)} %get-tuple-element.89), channel_id=1, source_target_pairs={{0,24},{4,28},{8,16},{12,20},{16,8},{20,12},{24,0},{28,4},{1,25},{... | collective-permute-start | bytes 491528 | tf_op jit(solution)/shard_map/ppermute | solution.py:488
  72.1 1.9 %collective-permute-start.21 = (f32[5,32,256]{2,1,0:T(8,128)S(1)}, f32[5,32,256]{2,1,0:T(8,128)S(1)}, u32[]{:S(2)}, u32[]{:S(2)}) collective-permute-start(f32[5,32,256]{2,1,0:T(8,128)S(1)} %get-tuple-element.91), channel_id=1, source_target_pairs={{0,8},{4,12},{8,0},{12,4},{16,24},{20,28},{24,16},{28,20},{1,9},{5... | collective-permute-start | bytes 491528 | tf_op jit(solution)/shard_map/ppermute | solution.py:488
  75.0 2.9 %collective-permute-start.12 = (f32[4,32,256]{2,1,0:T(8,128)S(1)}, f32[4,32,256]{2,1,0:T(8,128)S(1)}, u32[]{:S(2)}, u32[]{:S(2)}) collective-permute-start(f32[4,32,256]{2,1,0:T(8,128)S(1)} %get-tuple-element.75), channel_id=1, source_target_pairs={{0,28},{4,24},{8,12},{12,8},{16,20},{20,16},{24,4},{28,0},{1,29},{... | collective-permute-start | bytes 393224 | tf_op jit(solution)/shard_map/ppermute | solution.py:488
  79.6 2.5 %collective-permute-start.11 = (f32[5,32,256]{2,1,0:T(8,128)S(1)}, f32[5,32,256]{2,1,0:T(8,128)S(1)}, u32[]{:S(2)}, u32[]{:S(2)}) collective-permute-start(f32[5,32,256]{2,1,0:T(8,128)S(1)} %get-tuple-element.74), channel_id=1, source_target_pairs={{0,24},{4,28},{8,16},{12,20},{16,8},{20,12},{24,0},{28,4},{1,25},{... | collective-permute-start | bytes 491528 | tf_op jit(solution)/shard_map/ppermute | solution.py:488
  82.1 5.2 %collective-permute-done.12.refs_2_ = f32[4,32,256]{2,1,0:T(8,128)S(1)} collective-permute-done((f32[4,32,256]{2,1,0:T(8,128)S(1)}, f32[4,32,256]{2,1,0:T(8,128)S(1)}, u32[]{:S(2)}, u32[]{:S(2)}) %collective-permute-start.12) | collective-permute-done | bytes 131104 | tf_op jit(solution)/shard_map/ppermute | solution.py:488
  87.2 10.0 %collective-permute-start.13 = (f32[5,32,256]{2,1,0:T(8,128)S(1)}, f32[5,32,256]{2,1,0:T(8,128)S(1)}, u32[]{:S(2)}, u32[]{:S(2)}) collective-permute-start(f32[5,32,256]{2,1,0:T(8,128)S(1)} %get-tuple-element.76), channel_id=1, source_target_pairs={{0,16},{4,20},{8,24},{12,28},{16,0},{20,4},{24,8},{28,12},{1,17},{... | collective-permute-start | bytes 491528 | tf_op jit(solution)/shard_map/ppermute | solution.py:488
  97.4 3.3 %collective-permute-start.14 = (f32[4,32,256]{2,1,0:T(8,128)S(1)}, f32[4,32,256]{2,1,0:T(8,128)S(1)}, u32[]{:S(2)}, u32[]{:S(2)}) collective-permute-start(f32[4,32,256]{2,1,0:T(8,128)S(1)} %get-tuple-element.77), channel_id=1, source_target_pairs={{0,20},{4,16},{8,28},{12,24},{16,4},{20,0},{24,12},{28,8},{1,21},{... | collective-permute-start | bytes 393224 | tf_op jit(solution)/shard_map/ppermute | solution.py:488
  101.5 13.0 %collective-permute-done.14.refs_4_ = f32[4,32,256]{2,1,0:T(8,128)S(1)} collective-permute-done((f32[4,32,256]{2,1,0:T(8,128)S(1)}, f32[4,32,256]{2,1,0:T(8,128)S(1)}, u32[]{:S(2)}, u32[]{:S(2)}) %collective-permute-start.14) | collective-permute-done | bytes 131104 | tf_op jit(solution)/shard_map/ppermute | solution.py:488
  115.5 2.9 %collective-permute-start.24 = (f32[4,32,256]{2,1,0:T(8,128)S(1)}, f32[4,32,256]{2,1,0:T(8,128)S(1)}, u32[]{:S(2)}, u32[]{:S(2)}) collective-permute-start(f32[4,32,256]{2,1,0:T(8,128)S(1)} %get-tuple-element.94), channel_id=1, source_target_pairs={{0,28},{4,24},{8,12},{12,8},{16,20},{20,16},{24,4},{28,0},{1,29},{... | collective-permute-start | bytes 393224 | tf_op jit(solution)/shard_map/ppermute | solution.py:488
  118.5 2.8 %collective-permute-start.26 = (f32[4,32,256]{2,1,0:T(8,128)S(1)}, f32[4,32,256]{2,1,0:T(8,128)S(1)}, u32[]{:S(2)}, u32[]{:S(2)}) collective-permute-start(f32[4,32,256]{2,1,0:T(8,128)S(1)} %get-tuple-element.96), channel_id=1, source_target_pairs={{0,12},{4,8},{8,4},{12,0},{16,28},{20,24},{24,20},{28,16},{1,13},{... | collective-permute-start | bytes 393224 | tf_op jit(solution)/shard_map/ppermute | solution.py:488
  124.7 3.6 %collective-permute-done.25.refs_4_ = f32[4,32,256]{2,1,0:T(8,128)S(1)} collective-permute-done((f32[4,32,256]{2,1,0:T(8,128)S(1)}, f32[4,32,256]{2,1,0:T(8,128)S(1)}, u32[]{:S(2)}, u32[]{:S(2)}) %collective-permute-start.25) | collective-permute-done | bytes 131104 | tf_op jit(solution)/shard_map/ppermute | solution.py:488
  128.3 2.7 %collective-permute-done.22.message = f32[128,256]{1,0:T(8,128)S(1)} collective-permute-done((f32[128,256]{1,0:T(8,128)S(1)}, f32[128,256]{1,0:T(8,128)S(1)}, u32[]{:S(2)}, u32[]{:S(2)}) %collective-permute-start.22) | collective-permute-done | bytes 131104 | tf_op jit(solution)/shard_map/ppermute | solution.py:499
  131.0 12.2 %shard_map.91 = (f32[6,32,256]{2,1,0:T(8,128)S(1)}, f32[6,32,256]{2,1,0:T(8,128)S(1)}, f32[6,32,256]{2,1,0:T(8,128)S(1)}, f32[6,32,256]{2,1,0:T(8,128)S(1)}, f32...) custom-call(f32[256,512]{1,0:T(8,128)S(1)} %sine_select_fusion.basis, ...), custom_call_target="tpu_custom_call" | custom-call | flops 2415919104 | bytes 19144704 | tf_op jit(solution)/shard_map/pallas_call | solution.py:455
  144.2 2.5 %collective-permute-start.28 = (f32[6,32,256]{2,1,0:T(8,128)S(1)}, f32[6,32,256]{2,1,0:T(8,128)S(1)}, u32[]{:S(2)}, u32[]{:S(2)}) collective-permute-start(f32[6,32,256]{2,1,0:T(8,128)S(1)} %get-tuple-element.98), channel_id=1, source_target_pairs={{0,24},{4,28},{8,16},{12,20},{16,8},{20,12},{24,0},{28,4},{1,25},{... | collective-permute-start | bytes 589832 | tf_op jit(solution)/shard_map/ppermute | solution.py:488
  149.9 3.4 %collective-permute-start.31 = (f32[6,32,256]{2,1,0:T(8,128)S(1)}, f32[6,32,256]{2,1,0:T(8,128)S(1)}, u32[]{:S(2)}, u32[]{:S(2)}) collective-permute-start(f32[6,32,256]{2,1,0:T(8,128)S(1)} %get-tuple-element.101), channel_id=1, source_target_pairs={{0,20},{4,16},{8,28},{12,24},{16,4},{20,0},{24,12},{28,8},{1,21},{... | collective-permute-start | bytes 589832 | tf_op jit(solution)/shard_map/ppermute | solution.py:488
  153.3 14.7 %collective-permute-start.32 = (f32[6,32,256]{2,1,0:T(8,128)S(1)}, f32[6,32,256]{2,1,0:T(8,128)S(1)}, u32[]{:S(2)}, u32[]{:S(2)}) collective-permute-start(f32[6,32,256]{2,1,0:T(8,128)S(1)} %get-tuple-element.102), channel_id=1, source_target_pairs={{0,8},{4,12},{8,0},{12,4},{16,24},{20,28},{24,16},{28,20},{1,9},{5... | collective-permute-start | bytes 589832 | tf_op jit(solution)/shard_map/ppermute | solution.py:488
  168.0 4.2 %collective-permute-start.33 = (f32[6,32,256]{2,1,0:T(8,128)S(1)}, f32[6,32,256]{2,1,0:T(8,128)S(1)}, u32[]{:S(2)}, u32[]{:S(2)}) collective-permute-start(f32[6,32,256]{2,1,0:T(8,128)S(1)} %get-tuple-element.103), channel_id=1, source_target_pairs={{0,12},{4,8},{8,4},{12,0},{16,28},{20,24},{24,20},{28,16},{1,13},{... | collective-permute-start | bytes 589832 | tf_op jit(solution)/shard_map/ppermute | solution.py:488
  172.2 4.4 %shard_map.89 = (f32[3,16,32,256]{3,2,1,0:T(8,128)S(1)}, f32[3,32,16,256]{3,2,1,0:T(8,128)}) custom-call(f32[3,16,32,256]{3,2,1,0:T(8,128)S(1)} %get-tuple-element.81.e_zk, f32[3,16,32,256]{3,2,1,0:T(8,128)S(1)} %get-tuple-element.58.ahead, f32[3,16,32,256]{3,2,1,0:T(8,128)S(1)} %get-tuple-element.59.h_zk, f32[3,32,256]{2,1,0:T(8,128)S(1)} %collective-permute-done.17.above, ...), custom_call_target="tpu_custom_call" | custom-call | bytes 8159232 | tf_op jit(solution)/shard_map/pallas_call | solution.py:455
  178.2 2.7 %collective-permute-done.32.refs_5_ = f32[6,32,256]{2,1,0:T(8,128)S(1)} collective-permute-done((f32[6,32,256]{2,1,0:T(8,128)S(1)}, f32[6,32,256]{2,1,0:T(8,128)S(1)}, u32[]{:S(2)}, u32[]{:S(2)}) %collective-permute-start.32) | collective-permute-done | bytes 196640 | tf_op jit(solution)/shard_map/ppermute | solution.py:488
  180.9 2.6 %collective-permute-done.33.refs_6_ = f32[6,32,256]{2,1,0:T(8,128)S(1)} collective-permute-done((f32[6,32,256]{2,1,0:T(8,128)S(1)}, f32[6,32,256]{2,1,0:T(8,128)S(1)}, u32[]{:S(2)}, u32[]{:S(2)}) %collective-permute-start.33) | collective-permute-done | bytes 196640 | tf_op jit(solution)/shard_map/ppermute | solution.py:488
  (71 shorter events, 30.8 us)
Async XLA Ops:
  3.4 17.5 %collective-permute-start.2 = (f32[6,32,256]{2,1,0:T(8,128)}, f32[6,32,256]{2,1,0:T(8,128)S(1)}, u32[]{:S(2)}, u32[]{:S(2)}) collective-permute-start(f32[6,32,256]{2,1,0:T(8,128)} %get-tuple-element.60), channel_id=1, source_target_pairs={{0,4},{4,0},{8,20},{12,16},{16,12},{20,8},{24,28},{28,24},{1,5},{5... | collective-permute-start | bytes 589832 | tf_op jit(solution)/shard_map/ppermute | solution.py:488
  6.4 25.8 %collective-permute-start.3 = (f32[6,32,256]{2,1,0:T(8,128)}, f32[6,32,256]{2,1,0:T(8,128)}, u32[]{:S(2)}, u32[]{:S(2)}) collective-permute-start(f32[6,32,256]{2,1,0:T(8,128)} %get-tuple-element.61), channel_id=1, source_target_pairs={{0,24},{4,28},{8,16},{12,20},{16,8},{20,12},{24,0},{28,4},{1,25},{... | collective-permute-start | bytes 589832 | tf_op jit(solution)/shard_map/ppermute | solution.py:488
  10.0 28.7 %collective-permute-start.4 = (f32[6,32,256]{2,1,0:T(8,128)}, f32[6,32,256]{2,1,0:T(8,128)}, u32[]{:S(2)}, u32[]{:S(2)}) collective-permute-start(f32[6,32,256]{2,1,0:T(8,128)} %get-tuple-element.62), channel_id=1, source_target_pairs={{0,28},{4,24},{8,12},{12,8},{16,20},{20,16},{24,4},{28,0},{1,29},{... | collective-permute-start | bytes 589832 | tf_op jit(solution)/shard_map/ppermute | solution.py:488
  10.0 30.3 %collective-permute-start.5 = (f32[6,32,256]{2,1,0:T(8,128)}, f32[6,32,256]{2,1,0:T(8,128)}, u32[]{:S(2)}, u32[]{:S(2)}) collective-permute-start(f32[6,32,256]{2,1,0:T(8,128)} %get-tuple-element.63), channel_id=1, source_target_pairs={{0,16},{4,20},{8,24},{12,28},{16,0},{20,4},{24,8},{28,12},{1,17},{... | collective-permute-start | bytes 589832 | tf_op jit(solution)/shard_map/ppermute | solution.py:488
  11.0 32.4 %collective-permute-start.6 = (f32[6,32,256]{2,1,0:T(8,128)}, f32[6,32,256]{2,1,0:T(8,128)}, u32[]{:S(2)}, u32[]{:S(2)}) collective-permute-start(f32[6,32,256]{2,1,0:T(8,128)} %get-tuple-element.64), channel_id=1, source_target_pairs={{0,20},{4,16},{8,28},{12,24},{16,4},{20,0},{24,12},{28,8},{1,21},{... | collective-permute-start | bytes 589832 | tf_op jit(solution)/shard_map/ppermute | solution.py:488
  20.9 24.8 %collective-permute-start.7 = (f32[6,32,256]{2,1,0:T(8,128)}, f32[6,32,256]{2,1,0:T(8,128)S(1)}, u32[]{:S(2)}, u32[]{:S(2)}) collective-permute-start(f32[6,32,256]{2,1,0:T(8,128)} %get-tuple-element.65), channel_id=1, source_target_pairs={{0,8},{4,12},{8,0},{12,4},{16,24},{20,28},{24,16},{28,20},{1,9},{5... | collective-permute-start | bytes 589832 | tf_op jit(solution)/shard_map/ppermute | solution.py:488
  32.2 16.8 %collective-permute-start.8 = (f32[6,32,256]{2,1,0:T(8,128)}, f32[6,32,256]{2,1,0:T(8,128)S(1)}, u32[]{:S(2)}, u32[]{:S(2)}) collective-permute-start(f32[6,32,256]{2,1,0:T(8,128)} %get-tuple-element.66), channel_id=1, source_target_pairs={{0,12},{4,8},{8,4},{12,0},{16,28},{20,24},{24,20},{28,16},{1,13},{... | collective-permute-start | bytes 589832 | tf_op jit(solution)/shard_map/ppermute | solution.py:488
  38.7 27.3 %collective-permute-start.1 = (f32[2,3,32,256]{3,2,1,0:T(8,128)}, f32[2,3,32,256]{3,2,1,0:T(8,128)S(1)}, u32[]{:S(2)}, u32[]{:S(2)}) collective-permute-start(f32[2,3,32,256]{3,2,1,0:T(8,128)} %get-tuple-element.57), channel_id=1, source_target_pairs={{0,1},{1,2},{2,3},{4,5},{5,6},{6,7},{8,9},{9,10},{10,11},{12,13},{... | collective-permute-start | bytes 589832 | tf_op jit(solution)/shard_map/ppermute | solution.py:495
  61.7 13.3 %collective-permute-start.10 = (f32[128,256]{1,0:T(8,128)S(1)}, f32[128,256]{1,0:T(8,128)S(1)}, u32[]{:S(2)}, u32[]{:S(2)}) collective-permute-start(f32[128,256]{1,0:T(8,128)S(1)} %get-tuple-element.69), channel_id=1, source_target_pairs={{0,4},{4,0},{8,12},{12,8},{16,20},{20,16},{24,28},{28,24},{1,5},{5... | collective-permute-start | bytes 393224 | tf_op jit(solution)/shard_map/ppermute | solution.py:499
  69.6 27.7 %collective-permute-start.19 = (f32[5,32,256]{2,1,0:T(8,128)S(1)}, f32[5,32,256]{2,1,0:T(8,128)S(1)}, u32[]{:S(2)}, u32[]{:S(2)}) collective-permute-start(f32[5,32,256]{2,1,0:T(8,128)S(1)} %get-tuple-element.89), channel_id=1, source_target_pairs={{0,24},{4,28},{8,16},{12,20},{16,8},{20,12},{24,0},{28,4},{1,25},{... | collective-permute-start | bytes 491528 | tf_op jit(solution)/shard_map/ppermute | solution.py:488
  72.1 25.3 %collective-permute-start.20 = (f32[5,32,256]{2,1,0:T(8,128)S(1)}, f32[5,32,256]{2,1,0:T(8,128)S(1)}, u32[]{:S(2)}, u32[]{:S(2)}) collective-permute-start(f32[5,32,256]{2,1,0:T(8,128)S(1)} %get-tuple-element.90), channel_id=1, source_target_pairs={{0,16},{4,20},{8,24},{12,28},{16,0},{20,4},{24,8},{28,12},{1,17},{... | collective-permute-start | bytes 491528 | tf_op jit(solution)/shard_map/ppermute | solution.py:488
  72.1 28.6 %collective-permute-start.21 = (f32[5,32,256]{2,1,0:T(8,128)S(1)}, f32[5,32,256]{2,1,0:T(8,128)S(1)}, u32[]{:S(2)}, u32[]{:S(2)}) collective-permute-start(f32[5,32,256]{2,1,0:T(8,128)S(1)} %get-tuple-element.91), channel_id=1, source_target_pairs={{0,8},{4,12},{8,0},{12,4},{16,24},{20,28},{24,16},{28,20},{1,9},{5... | collective-permute-start | bytes 491528 | tf_op jit(solution)/shard_map/ppermute | solution.py:488
  74.0 5.6 %collective-permute-start.9 = (f32[4,32,256]{2,1,0:T(8,128)S(1)}, f32[4,32,256]{2,1,0:T(8,128)S(1)}, u32[]{:S(2)}, u32[]{:S(2)}) collective-permute-start(f32[4,32,256]{2,1,0:T(8,128)S(1)} %get-tuple-element.68), channel_id=1, source_target_pairs={{0,4},{4,0},{8,20},{12,16},{16,12},{20,8},{24,28},{28,24},{1,5},{5... | collective-permute-start | bytes 393224 | tf_op jit(solution)/shard_map/ppermute | solution.py:488
  75.0 12.2 %collective-permute-start.12 = (f32[4,32,256]{2,1,0:T(8,128)S(1)}, f32[4,32,256]{2,1,0:T(8,128)S(1)}, u32[]{:S(2)}, u32[]{:S(2)}) collective-permute-start(f32[4,32,256]{2,1,0:T(8,128)S(1)} %get-tuple-element.75), channel_id=1, source_target_pairs={{0,28},{4,24},{8,12},{12,8},{16,20},{20,16},{24,4},{28,0},{1,29},{... | collective-permute-start | bytes 393224 | tf_op jit(solution)/shard_map/ppermute | solution.py:488
  79.6 38.9 %collective-permute-start.11 = (f32[5,32,256]{2,1,0:T(8,128)S(1)}, f32[5,32,256]{2,1,0:T(8,128)S(1)}, u32[]{:S(2)}, u32[]{:S(2)}) collective-permute-start(f32[5,32,256]{2,1,0:T(8,128)S(1)} %get-tuple-element.74), channel_id=1, source_target_pairs={{0,24},{4,28},{8,16},{12,20},{16,8},{20,12},{24,0},{28,4},{1,25},{... | collective-permute-start | bytes 491528 | tf_op jit(solution)/shard_map/ppermute | solution.py:488
  87.2 31.2 %collective-permute-start.13 = (f32[5,32,256]{2,1,0:T(8,128)S(1)}, f32[5,32,256]{2,1,0:T(8,128)S(1)}, u32[]{:S(2)}, u32[]{:S(2)}) collective-permute-start(f32[5,32,256]{2,1,0:T(8,128)S(1)} %get-tuple-element.76), channel_id=1, source_target_pairs={{0,16},{4,20},{8,24},{12,28},{16,0},{20,4},{24,8},{28,12},{1,17},{... | collective-permute-start | bytes 491528 | tf_op jit(solution)/shard_map/ppermute | solution.py:488
  97.2 24.0 %collective-permute-start.15 = (f32[5,32,256]{2,1,0:T(8,128)S(1)}, f32[5,32,256]{2,1,0:T(8,128)S(1)}, u32[]{:S(2)}, u32[]{:S(2)}) collective-permute-start(f32[5,32,256]{2,1,0:T(8,128)S(1)} %get-tuple-element.78), channel_id=1, source_target_pairs={{0,8},{4,12},{8,0},{12,4},{16,24},{20,28},{24,16},{28,20},{1,9},{5... | collective-permute-start | bytes 491528 | tf_op jit(solution)/shard_map/ppermute | solution.py:488
  97.4 17.1 %collective-permute-start.14 = (f32[4,32,256]{2,1,0:T(8,128)S(1)}, f32[4,32,256]{2,1,0:T(8,128)S(1)}, u32[]{:S(2)}, u32[]{:S(2)}) collective-permute-start(f32[4,32,256]{2,1,0:T(8,128)S(1)} %get-tuple-element.77), channel_id=1, source_target_pairs={{0,20},{4,16},{8,28},{12,24},{16,4},{20,0},{24,12},{28,8},{1,21},{... | collective-permute-start | bytes 393224 | tf_op jit(solution)/shard_map/ppermute | solution.py:488
  100.7 14.8 %collective-permute-start.16 = (f32[4,32,256]{2,1,0:T(8,128)S(1)}, f32[4,32,256]{2,1,0:T(8,128)S(1)}, u32[]{:S(2)}, u32[]{:S(2)}) collective-permute-start(f32[4,32,256]{2,1,0:T(8,128)S(1)} %get-tuple-element.79), channel_id=1, source_target_pairs={{0,12},{4,8},{8,4},{12,0},{16,28},{20,24},{24,20},{28,16},{1,13},{... | collective-permute-start | bytes 393224 | tf_op jit(solution)/shard_map/ppermute | solution.py:488
  114.5 8.0 %collective-permute-start.23 = (f32[4,32,256]{2,1,0:T(8,128)S(1)}, f32[4,32,256]{2,1,0:T(8,128)S(1)}, u32[]{:S(2)}, u32[]{:S(2)}) collective-permute-start(f32[4,32,256]{2,1,0:T(8,128)S(1)} %get-tuple-element.93), channel_id=1, source_target_pairs={{0,4},{4,0},{8,20},{12,16},{16,12},{20,8},{24,28},{28,24},{1,5},{5... | collective-permute-start | bytes 393224 | tf_op jit(solution)/shard_map/ppermute | solution.py:488
  115.5 9.2 %collective-permute-start.24 = (f32[4,32,256]{2,1,0:T(8,128)S(1)}, f32[4,32,256]{2,1,0:T(8,128)S(1)}, u32[]{:S(2)}, u32[]{:S(2)}) collective-permute-start(f32[4,32,256]{2,1,0:T(8,128)S(1)} %get-tuple-element.94), channel_id=1, source_target_pairs={{0,28},{4,24},{8,12},{12,8},{16,20},{20,16},{24,4},{28,0},{1,29},{... | collective-permute-start | bytes 393224 | tf_op jit(solution)/shard_map/ppermute | solution.py:488
  118.5 9.9 %collective-permute-start.25 = (f32[4,32,256]{2,1,0:T(8,128)S(1)}, f32[4,32,256]{2,1,0:T(8,128)S(1)}, u32[]{:S(2)}, u32[]{:S(2)}) collective-permute-start(f32[4,32,256]{2,1,0:T(8,128)S(1)} %get-tuple-element.95), channel_id=1, source_target_pairs={{0,20},{4,16},{8,28},{12,24},{16,4},{20,0},{24,12},{28,8},{1,21},{... | collective-permute-start | bytes 393224 | tf_op jit(solution)/shard_map/ppermute | solution.py:488
  118.5 9.8 %collective-permute-start.26 = (f32[4,32,256]{2,1,0:T(8,128)S(1)}, f32[4,32,256]{2,1,0:T(8,128)S(1)}, u32[]{:S(2)}, u32[]{:S(2)}) collective-permute-start(f32[4,32,256]{2,1,0:T(8,128)S(1)} %get-tuple-element.96), channel_id=1, source_target_pairs={{0,12},{4,8},{8,4},{12,0},{16,28},{20,24},{24,20},{28,16},{1,13},{... | collective-permute-start | bytes 393224 | tf_op jit(solution)/shard_map/ppermute | solution.py:488
  121.3 9.8 %collective-permute-start.22 = (f32[128,256]{1,0:T(8,128)S(1)}, f32[128,256]{1,0:T(8,128)S(1)}, u32[]{:S(2)}, u32[]{:S(2)}) collective-permute-start(f32[128,256]{1,0:T(8,128)S(1)} %shard_map.90), channel_id=1, source_target_pairs={{0,4},{4,0},{8,12},{12,8},{16,20},{20,16},{24,28},{28,24},{1,5},{5... | collective-permute-start | bytes 393224 | tf_op jit(solution)/shard_map/ppermute | solution.py:499
  122.5 27.4 %collective-permute-start.18 = (f32[2,3,32,256]{3,2,1,0:T(8,128)S(1)}, f32[2,3,32,256]{3,2,1,0:T(8,128)S(1)}, u32[]{:S(2)}, u32[]{:S(2)}) collective-permute-start(f32[2,3,32,256]{3,2,1,0:T(8,128)S(1)} %get-tuple-element.83), channel_id=1, source_target_pairs={{0,1},{1,2},{2,3},{4,5},{5,6},{6,7},{8,9},{9,10},{10,11},{12,13},{... | collective-permute-start | bytes 589832 | tf_op jit(solution)/shard_map/ppermute | solution.py:495
  143.2 10.1 %collective-permute-start.27 = (f32[6,32,256]{2,1,0:T(8,128)S(1)}, f32[6,32,256]{2,1,0:T(8,128)S(1)}, u32[]{:S(2)}, u32[]{:S(2)}) collective-permute-start(f32[6,32,256]{2,1,0:T(8,128)S(1)} %get-tuple-element.97), channel_id=1, source_target_pairs={{0,4},{4,0},{8,20},{12,16},{16,12},{20,8},{24,28},{28,24},{1,5},{5... | collective-permute-start | bytes 589832 | tf_op jit(solution)/shard_map/ppermute | solution.py:488
  144.2 23.7 %collective-permute-start.28 = (f32[6,32,256]{2,1,0:T(8,128)S(1)}, f32[6,32,256]{2,1,0:T(8,128)S(1)}, u32[]{:S(2)}, u32[]{:S(2)}) collective-permute-start(f32[6,32,256]{2,1,0:T(8,128)S(1)} %get-tuple-element.98), channel_id=1, source_target_pairs={{0,24},{4,28},{8,16},{12,20},{16,8},{20,12},{24,0},{28,4},{1,25},{... | collective-permute-start | bytes 589832 | tf_op jit(solution)/shard_map/ppermute | solution.py:488
  148.0 28.5 %collective-permute-start.29 = (f32[6,32,256]{2,1,0:T(8,128)S(1)}, f32[6,32,256]{2,1,0:T(8,128)S(1)}, u32[]{:S(2)}, u32[]{:S(2)}) collective-permute-start(f32[6,32,256]{2,1,0:T(8,128)S(1)} %get-tuple-element.99), channel_id=1, source_target_pairs={{0,28},{4,24},{8,12},{12,8},{16,20},{20,16},{24,4},{28,0},{1,29},{... | collective-permute-start | bytes 589832 | tf_op jit(solution)/shard_map/ppermute | solution.py:488
  149.9 26.6 %collective-permute-start.30 = (f32[6,32,256]{2,1,0:T(8,128)S(1)}, f32[6,32,256]{2,1,0:T(8,128)S(1)}, u32[]{:S(2)}, u32[]{:S(2)}) collective-permute-start(f32[6,32,256]{2,1,0:T(8,128)S(1)} %get-tuple-element.100), channel_id=1, source_target_pairs={{0,16},{4,20},{8,24},{12,28},{16,0},{20,4},{24,8},{28,12},{1,17},{... | collective-permute-start | bytes 589832 | tf_op jit(solution)/shard_map/ppermute | solution.py:488
  149.9 28.3 %collective-permute-start.31 = (f32[6,32,256]{2,1,0:T(8,128)S(1)}, f32[6,32,256]{2,1,0:T(8,128)S(1)}, u32[]{:S(2)}, u32[]{:S(2)}) collective-permute-start(f32[6,32,256]{2,1,0:T(8,128)S(1)} %get-tuple-element.101), channel_id=1, source_target_pairs={{0,20},{4,16},{8,28},{12,24},{16,4},{20,0},{24,12},{28,8},{1,21},{... | collective-permute-start | bytes 589832 | tf_op jit(solution)/shard_map/ppermute | solution.py:488
  153.3 27.6 %collective-permute-start.32 = (f32[6,32,256]{2,1,0:T(8,128)S(1)}, f32[6,32,256]{2,1,0:T(8,128)S(1)}, u32[]{:S(2)}, u32[]{:S(2)}) collective-permute-start(f32[6,32,256]{2,1,0:T(8,128)S(1)} %get-tuple-element.102), channel_id=1, source_target_pairs={{0,8},{4,12},{8,0},{12,4},{16,24},{20,28},{24,16},{28,20},{1,9},{5... | collective-permute-start | bytes 589832 | tf_op jit(solution)/shard_map/ppermute | solution.py:488
  168.0 15.5 %collective-permute-start.33 = (f32[6,32,256]{2,1,0:T(8,128)S(1)}, f32[6,32,256]{2,1,0:T(8,128)S(1)}, u32[]{:S(2)}, u32[]{:S(2)}) collective-permute-start(f32[6,32,256]{2,1,0:T(8,128)S(1)} %get-tuple-element.103), channel_id=1, source_target_pairs={{0,12},{4,8},{8,4},{12,0},{16,28},{20,24},{24,20},{28,16},{1,13},{... | collective-permute-start | bytes 589832 | tf_op jit(solution)/shard_map/ppermute | solution.py:488
  (9 other events, 129.3 us)
